TPU v7x, 32 devices: a whole 2x2x4 slice. The times are simulated.
32 devices in a mesh: dp: 8 (over z, x), mp: 4 (over y, core).
Axes of the slice: x: 2, y: 2, z: 4, core: 2. Of those that a mesh axis runs over, the one named last changes fastest.
Arguments:
- tokens: bfloat16 [2, 16384, 768], P(None, ('dp', 'mp')), may hold values from -6 to 6
- segment_ids: int32 [2, 16384], P(None, 'dp'), may hold values from 0 to 63, never falling along the last dimension, each value on 1 to 768 neighbouring positions
- norm1_gain: float32 [768], replicated, may hold values from 0.1 to 1.9
- norm1_bias: float32 [768], replicated, may hold values from -3 to 3
- w_qkv: bfloat16 [768, 3, 768], replicated, may hold values from -0.21875 to 0.21875
- conv_weight: float32 [3, 3, 768], P(None, None, 'mp'), may hold values from -3 to 3
- w_out: bfloat16 [768, 768], replicated, may hold values from -1.75 to 1.75
- norm2_gain: float32 [768], replicated, may hold values from 0.1 to 1.9
- norm2_bias: float32 [768], replicated, may hold values from -3 to 3
- w_in: bfloat16 [768, 3072], replicated, may hold values from -0.21875 to 0.21875
- w_down: bfloat16 [3072, 768], replicated, may hold values from -0.109375 to 0.109375
- cotangent: bfloat16 [2, 16384, 768], P(None, ('dp', 'mp')), may hold values from -6 to 6
Outputs:
- output: bfloat16 [2, 16384, 768], P(None, ('dp', 'mp'))
- input_grad: float32 [2, 16384, 768], P(None, ('dp', 'mp'))
- norm1_gain_grad: float32 [768], P('mp')
- norm1_bias_grad: float32 [768], P('mp')
- qkv_grad: float32 [768, 3, 768], P(None, None, 'mp')
- conv_grad: float32 [3, 3, 768], P(None, None, 'mp')
- out_grad: float32 [768, 768], P('mp')
- norm2_gain_grad: float32 [768], P('mp')
- norm2_bias_grad: float32 [768], P('mp')
- in_grad: float32 [768, 3072], replicated
- down_grad: float32 [3072, 768], replicated
Inputs may be any that keep to these rules, and one draw needn't show every extreme that they name: `segment_ids`: segment numbers never fall along a row of 16384 tokens. A document may run on past the end of a sequence of 1024 tokens, but attention and the convolution still stop there, whatever the numbers.
All inputs are finite; a program needn't handle non-finite values.
Results may differ from a plain program's by a relative error of at most 0.015.
The roundings to bfloat16 on the way count: a program that leaves them out, or rounds other values in their place, can miss the bound.
Values may be sent and summed in bfloat16 or wider, within the bound.
No kernel may reach another device: no remote copies, remote signals or barrier semaphores. Data moves between devices by JAX's collectives and lax.ppermute only.
A program may use at most 256 MiB of HBM per device.

v0:
```python
import functools
import math

import jax
import jax.numpy as jnp
from jax import lax
from jax.experimental import pallas as pl
from jax.experimental.pallas import tpu as pltpu
from jax.sharding import PartitionSpec as P

HEAD_DIM = 64
LEN = 1024
LANES = 128
BLOCK = 256
FEED_ROWS = 256
EPSILON = 1e-05
MASKED = -1e30
F32 = jnp.float32
BF16 = jnp.bfloat16


def dot(a, b, dims):
    return lax.dot_general(a, b, (dims, ((), ())), preferred_element_type=F32)


def normalize(values, norm_gain, norm_bias):
    centred = values - jnp.mean(values, axis=-1, keepdims=True)
    rstd_row = lax.rsqrt(jnp.mean(centred * centred, axis=-1, keepdims=True) + EPSILON)
    scaled = centred * rstd_row
    return (scaled * norm_gain + norm_bias, scaled, rstd_row)


def normalize_back(gradient, scaled, rstd_row, norm_gain):
    grad_scaled = gradient * norm_gain
    inner_term = (
        grad_scaled
        - jnp.mean(grad_scaled, axis=-1, keepdims=True)
        - scaled * jnp.mean(grad_scaled * scaled, axis=-1, keepdims=True)
    )
    return (rstd_row * inner_term, jnp.sum(gradient * scaled, axis=0), jnp.sum(gradient, axis=0))


def attend_kernel(
    place, proj_q, proj_k, proj_v, taps, segments, mixed_out, attended, lse, same, seg_col, seg_row, bias
):
    q_out, k_out, v_out = mixed_out.at[0], mixed_out.at[1], mixed_out.at[2]

    @pl.when(pl.program_id(0) == 0)
    def _():
        numbers = jnp.where(place[0] == 0, segments[0:1, :], segments[1:2, :])
        seg_row[...] = jnp.broadcast_to(numbers, seg_row.shape)
        column = jnp.broadcast_to(numbers.astype(F32), (LANES, LEN)).T
        seg_col[...] = column.astype(jnp.int32)
        at = lax.broadcasted_iota(jnp.int32, (LEN, LANES), 0)
        for shift in (1, 2):
            equal = (at >= shift) & (pltpu.roll(column, shift, 0) == column)
            same[shift - 1] = jnp.where(equal, 1.0, 0.0)
        for first in range(0, LEN, BLOCK):
            width = first + BLOCK
            rows = first + lax.broadcasted_iota(jnp.int32, (BLOCK, width), 0)
            cols = lax.broadcasted_iota(jnp.int32, (BLOCK, width), 1)
            mine = jnp.concatenate([seg_col[first:width, :]] * (width // LANES), axis=1)
            allowed = (cols <= rows) & (mine == seg_row[0:1, :width])
            bias[first:width, :width] = jnp.where(allowed, 0.0, MASKED)

    same_one, same_two = same[0], same[1]
    for which, (source, target) in enumerate(((proj_q, q_out), (proj_k, k_out), (proj_v, v_out))):
        values = source[...].astype(F32)
        mixed = (
            values * taps[3 * which : 3 * which + 1, :]
            + pltpu.roll(values, 1, 0) * same_one * taps[3 * which + 1 : 3 * which + 2, :]
            + pltpu.roll(values, 2, 0) * same_two * taps[3 * which + 2 : 3 * which + 3, :]
        )
        target[...] = mixed.astype(BF16)
    scaling = 1.0 / math.sqrt(HEAD_DIM)
    lane = lax.broadcasted_iota(jnp.int32, (1, LANES), 1)
    for first in range(0, LEN, BLOCK):
        width = first + BLOCK
        queries = q_out[first:width, :] * jnp.asarray(scaling, BF16)
        parts = []
        for head in range(2):
            chosen = (lane >= HEAD_DIM) if head else (lane < HEAD_DIM)
            mine = jnp.where(chosen, queries, jnp.zeros_like(queries))
            scores = dot(mine, k_out[:width, :], ((1,), (1,))) + bias[first:width, :width]
            top = jnp.max(scores, axis=1, keepdims=True)
            weights = jnp.exp(scores - top)
            total = jnp.sum(weights, axis=1, keepdims=True)
            product = dot(weights.astype(BF16), v_out[:width, :], ((1,), (0,)))
            parts.append((product * (1.0 / total), top + jnp.log(total)))
        left = lane < HEAD_DIM
        attended[first:width, :] = jnp.where(left, parts[0][0], parts[1][0]).astype(BF16)
        logs = jnp.where(left, parts[0][1], parts[1][1])
        flipped = logs.T
        lse[0:1, first:width] = flipped[0:1, :]
        lse[1:2, first:width] = flipped[HEAD_DIM : HEAD_DIM + 1, :]


def attend_back_kernel(
    continued,
    *refs,
):
    attend_back_body(*(refs[2:] if continued else refs))


def attend_back_body(
    mixed_in,
    grads,
    attended,
    lse,
    proj_q,
    proj_k,
    proj_v,
    taps,
    same,
    seg_col,
    seg_row,
    back,
    tap_grads,
    bias,
    grad_k,
    grad_v,
    grad_qt,
    keys_t,
    inner,
):
    q_in, k_in, v_in = mixed_in.at[0], mixed_in.at[1], mixed_in.at[2]
    back_q, back_k, back_v = back.at[0], back.at[1], back.at[2]

    @pl.when(pl.program_id(0) == 0)
    def _():
        for first in range(0, LEN, BLOCK):
            width = first + BLOCK
            rows = lax.broadcasted_iota(jnp.int32, (width, BLOCK), 0)
            cols = first + lax.broadcasted_iota(jnp.int32, (width, BLOCK), 1)
            theirs = jnp.concatenate([seg_col[:width, :]] * (BLOCK // LANES), axis=1)
            allowed = (rows <= cols) & (theirs == seg_row[0:1, first:width])
            bias[:width, first:width] = jnp.where(allowed, 0.0, MASKED)

    scaling = 1.0 / math.sqrt(HEAD_DIM)
    lane = lax.broadcasted_iota(jnp.int32, (1, LANES), 1)
    keys_t[...] = k_in[...].T
    inner[...] = (grads[...].astype(F32) * attended[...].astype(F32)).T
    grad_k[...] = jnp.zeros_like(grad_k)
    grad_v[...] = jnp.zeros_like(grad_v)

    def one_head(head, _):
        low = pl.multiple_of(head * HEAD_DIM, HEAD_DIM)
        mine = pl.ds(low, HEAD_DIM)
        chosen = (lane >= low) & (lane < low + HEAD_DIM)
        inner_row = jnp.sum(inner[mine, :], axis=0, keepdims=True)
        for first in range(0, LEN, BLOCK):
            width = first + BLOCK
            queries = q_in[first:width, :] * jnp.asarray(scaling, BF16)
            queries = jnp.where(chosen, queries, jnp.zeros_like(queries))
            outer = grads[first:width, :]
            outer = jnp.where(chosen, outer, jnp.zeros_like(outer))
            scores = dot(k_in[:width, :], queries, ((1,), (1,))) + bias[:width, first:width]
            probs = jnp.exp(scores - lse[pl.ds(head, 1), first:width])
            grad_probs = dot(v_in[:width, :], outer, ((1,), (1,)))
            grad_scores = (probs * (grad_probs - inner_row[:, first:width])).astype(BF16)
            grad_v[:width, :] += dot(probs.astype(BF16), outer, ((1,), (0,)))
            grad_k[:width, :] += dot(grad_scores, queries, ((1,), (0,)))
            grad_qt[mine, first:width] = dot(keys_t[mine, :width], grad_scores, ((1,), (0,)))
        return 0

    lax.fori_loop(0, 2, one_head, 0)
    same_one, same_two = same[0], same[1]
    grad_q = grad_qt[...].T * scaling
    for which, (gradient, source, target) in enumerate(
        ((grad_q, proj_q, back_q), (grad_k[...], proj_k, back_k), (grad_v[...], proj_v, back_v))
    ):
        values = source[...].astype(F32)
        row = 3 * which
        after_one = pltpu.roll(gradient * same_one, LEN - 1, 0)
        after_two = pltpu.roll(gradient * same_two, LEN - 2, 0)
        tap_grads[row : row + 1, :] = jnp.sum(gradient * values, axis=0, keepdims=True)
        tap_grads[row + 1 : row + 2, :] = jnp.sum(after_one * values, axis=0, keepdims=True)
        tap_grads[row + 2 : row + 3, :] = jnp.sum(after_two * values, axis=0, keepdims=True)
        target[...] = (
            gradient * taps[row : row + 1, :]
            + after_one * taps[row + 1 : row + 2, :]
            + after_two * taps[row + 2 : row + 3, :]
        ).astype(BF16)


def whole(shape):
    return pl.BlockSpec(shape, lambda *_: (0,) * len(shape))


def cost(flops, moved, exps=0):
    return pl.CostEstimate(flops=int(flops), transcendentals=int(exps), bytes_accessed=int(moved))


def attend(place, projected, taps, segments):
    width = projected.shape[1] // 3
    pairs = width // LANES

    def column(offset):
        return pl.BlockSpec((LEN, LANES), lambda h, s, offset=offset: (0, offset + h))

    return pl.pallas_call(
        attend_kernel,
        grid_spec=pltpu.PrefetchScalarGridSpec(
            num_scalar_prefetch=1,
            grid=(pairs,),
            in_specs=[
                column(0),
                column(pairs),
                column(2 * pairs),
                pl.BlockSpec((9, LANES), lambda h, s: (0, h)),
                pl.BlockSpec((2, LEN), lambda h, s: (0, s[3])),
            ],
            out_specs=[
                pl.BlockSpec((3, LEN, LANES), lambda h, s: (0, 0, h)),
                column(0),
                pl.BlockSpec((None, 2, LEN), lambda h, s: (h, 0, 0)),
                whole((2, LEN, LANES)),
                whole((LEN, LANES)),
                whole((8, LEN)),
            ],
            scratch_shapes=[pltpu.VMEM((LEN, LEN), F32)],
        ),
        out_shape=[
            jax.ShapeDtypeStruct((3, LEN, width), BF16),
            jax.ShapeDtypeStruct((LEN, width), BF16),
            jax.ShapeDtypeStruct((pairs, 2, LEN), F32),
            jax.ShapeDtypeStruct((2, LEN, LANES), F32),
            jax.ShapeDtypeStruct((LEN, LANES), jnp.int32),
            jax.ShapeDtypeStruct((8, LEN), jnp.int32),
        ],
        cost_estimate=cost(4 * LEN * LEN * width, 16 * LEN * width, LEN * LEN * pairs),
        name="attend",
    )(place, projected, projected, projected, taps, segments)


def attend_back(first_pair, pairs, so_far, mixed, grads, attended, lse, projected, taps, same, seg_col, seg_row):
    width = grads.shape[1]
    all_pairs = width // LANES

    def column(offset):
        return pl.BlockSpec((LEN, LANES), lambda h, offset=offset: (0, first_pair + offset + h))

    stack = pl.BlockSpec((3, LEN, LANES), lambda h: (0, 0, first_pair + h))
    rows = pl.BlockSpec((9, LANES), lambda h: (0, first_pair + h))
    there = [pl.BlockSpec(memory_space=pl.ANY)] * 2 if so_far else []
    taken = pairs * LANES
    return pl.pallas_call(
        functools.partial(attend_back_kernel, bool(so_far)),
        grid=(pairs,),
        in_specs=there
        + [
            stack,
            column(0),
            column(0),
            pl.BlockSpec((None, 2, LEN), lambda h: (first_pair + h, 0, 0)),
            column(0),
            column(all_pairs),
            column(2 * all_pairs),
            rows,
            whole((2, LEN, LANES)),
            whole((LEN, LANES)),
            whole((8, LEN)),
        ],
        out_specs=[stack, rows],
        out_shape=[
            jax.ShapeDtypeStruct((3, LEN, width), BF16),
            jax.ShapeDtypeStruct((9, width), F32),
        ],
        scratch_shapes=[
            pltpu.VMEM((LEN, LEN), F32),
            pltpu.VMEM((LEN, LANES), F32),
            pltpu.VMEM((LEN, LANES), F32),
            pltpu.VMEM((LANES, LEN), F32),
            pltpu.VMEM((LANES, LEN), BF16),
            pltpu.VMEM((LANES, LEN), F32),
        ],
        input_output_aliases={0: 0, 1: 1} if so_far else {},
        cost_estimate=cost(10 * LEN * LEN * taken, 22 * LEN * taken, LEN * LEN * pairs),
        name="attend_back",
    )(*so_far, mixed, grads, attended, lse, projected, projected, projected, taps, same, seg_col, seg_row)


def front_kernel(continued, place, *refs):
    tokens, gain, offset, weights, projected, normed, rows_out = refs[3:] if continued else refs

    @pl.when(pl.program_id(0) == 0)
    def _():
        rows_out[...] = tokens[...]
        value, _, _ = normalize(tokens[...].astype(F32), row_of(gain), row_of(offset))
        normed[...] = value.astype(BF16)

    projected[...] = dot(normed[...], weights[...], ((1,), (0,))).astype(BF16)


def row_of(vector):
    return vector[...].reshape(1, vector.shape[0])


def front(place, tokens, gain, offset, weights, so_far):
    _, half, width = tokens.shape
    other = int(bool(so_far))
    mine = pl.BlockSpec((half, width), lambda j, s: (s[0] ^ other, 0))
    return pl.pallas_call(
        functools.partial(front_kernel, bool(so_far)),
        grid_spec=pltpu.PrefetchScalarGridSpec(
            num_scalar_prefetch=1,
            grid=(3,),
            in_specs=[pl.BlockSpec(memory_space=pl.ANY)] * len(so_far)
            + [
                pl.BlockSpec((None, half, width), lambda j, s: (s[0], 0, 0)),
                whole((width,)),
                whole((width,)),
                pl.BlockSpec((None, width, width), lambda j, s: (j, 0, 0)),
            ],
            out_specs=[pl.BlockSpec((half, width), lambda j, s: (s[0] ^ other, j)), mine, mine],
        ),
        out_shape=[
            jax.ShapeDtypeStruct((2 * half, 3 * width), BF16),
            jax.ShapeDtypeStruct((2 * half, width), BF16),
            jax.ShapeDtypeStruct((2 * half, width), BF16),
        ],
        input_output_aliases={1: 0, 2: 1, 3: 2} if so_far else {},
        cost_estimate=cost(6 * half * width * width, 14 * half * width + 6 * width * width),
        name="front",
    )(place, *so_far, tokens, gain, offset, weights)


def feed_kernel(number, other, first, last, place, *refs):
    core, here = place[0], place[1 + other]
    square = 2 * number + (core ^ other)
    if first:
        gain, offset, tokens, attended, w_out, mine, theirs, w_in, w_down = refs[:9]
        resid_out, normed_out, grads_out, parts_out, out, back_out = refs[9:15]
        tokens_held, attended_held, weights_held = refs[-3:]
        scratch = refs[15:-3]
    else:
        normed_in, out_in, back_in, grads_in, w_in, w_down = refs[:6]
        if last:
            parts_out, out_theirs, out_mine, back_out = refs[6:10]
            result_low = refs[-1]
            scratch = refs[10:-1]
        else:
            parts_out, out, back_out = refs[6:9]
            scratch = refs[9:]
    lefts, rights, in_block, down_block, total, back, parts, sems = scratch
    hidden, normed, grads, grad_pre = lefts.at[0], lefts.at[1], rights.at[0], rights.at[1]
    count = normed.shape[0]
    width = in_block.shape[1]
    half = normed.shape[0] // 2
    columns = pl.ds(pl.multiple_of(square * width, width), width)
    my_rows = pl.ds(pl.multiple_of(core * half, half), half)
    their_rows = pl.ds(pl.multiple_of((1 - core) * half, half), half)
    flights = []

    def copy(source, target):
        flight = pltpu.make_async_copy(source, target, sems.at[len(flights)])
        flights.append(flight)
        flight.start()
        return flight

    if first:
        early = [copy(attended, attended_held), copy(w_out, weights_held), copy(tokens, tokens_held)]
        later = [copy(w_in.at[:, columns], in_block)]
        last_in = [
            copy(mine.at[core], grads.at[my_rows, :]),
            copy(theirs.at[core], grads.at[their_rows, :]),
            copy(w_down.at[columns, :], down_block),
        ]
    else:
        early = [copy(normed_in, normed)]
        later = [copy(w_in.at[:, columns], in_block)]
        last_in = [copy(grads_in, grads), copy(w_down.at[columns, :], down_block)]
        total_in = copy(out_in, total)
        back_so_far = copy(back_in, back)
    for flight in early:
        flight.wait()
    writes = []
    if first:

        def begin(step, _):
            at = pl.ds(pl.multiple_of(step * BLOCK, BLOCK), BLOCK)
            product = dot(attended_held[at, :], weights_held[...], ((1,), (0,)))
            value = tokens_held[at, :].astype(F32) + product
            total[at, :] = value
            value, _, _ = normalize(value, row_of(gain), row_of(offset))
            normed[at, :] = value.astype(BF16)
            return 0

        lax.fori_loop(0, count // BLOCK, begin, 0)
        resid_flight = copy(total, resid_out)
        writes.append(copy(normed, normed_out))
    for flight in later + last_in:
        flight.wait()
    if first:
        writes.append(copy(grads, grads_out))
    size = FEED_ROWS

    def inner(step, _):
        at = pl.ds(pl.multiple_of(step * size, size), size)
        active = jnp.maximum(dot(normed[at, :], in_block[...], ((1,), (0,))), 0.0)
        hidden[at, :] = (active * active).astype(BF16)
        grad_hidden = dot(grads[at, :], down_block[...], ((1,), (1,)))
        grad_pre[at, :] = (grad_hidden * 2.0 * active).astype(BF16)
        return 0

    lax.fori_loop(0, count // size, inner, 0)
    blocks, _, rows, _ = parts.shape
    taken = width // 2

    def weigh(step, _):
        which, half_at = step // 2, step % 2
        at = pl.ds(pl.multiple_of(half_at * taken, taken), taken)
        product = dot(lefts[which, :, at], rights[which], ((0,), (0,))).astype(BF16)
        for index in range(blocks // 2):
            target = (half_at * (blocks // 2) + index) ^ here
            parts[target, which, :, :] = product[index * rows : (index + 1) * rows, :]
        return 0

    lax.fori_loop(0, 4, weigh, 0)
    writes.append(copy(parts, parts_out))
    if first:
        resid_flight.wait()
    else:
        total_in.wait()
        back_so_far.wait()

    def outer(step, _):
        at = pl.ds(pl.multiple_of(step * size, size), size)
        value = total[at, :] + dot(hidden[at, :], down_block[...], ((1,), (0,)))
        if last:
            result_low[at, :] = value.astype(BF16)
        else:
            total[at, :] = value
        product = dot(grad_pre[at, :], in_block[...], ((1,), (1,)))
        back[at, :] = product if first else back[at, :] + product
        return 0

    lax.fori_loop(0, count // size, outer, 0)
    if last:
        writes.append(copy(result_low.at[their_rows, :], out_theirs))
        writes.append(copy(result_low.at[my_rows, :], out_mine))
    else:
        writes.append(copy(total, out))
    writes.append(copy(back, back_out))
    for flight in writes:
        flight.wait()


def feed(number, other, last, place, ahead, w_in, w_down):
    first = len(ahead) == 7
    rows, width = ahead[2].shape
    sums = jax.ShapeDtypeStruct((rows, width), F32)
    low = jax.ShapeDtypeStruct((rows, width), BF16)
    half = jax.ShapeDtypeStruct((rows // 2, width), BF16)
    out_shape = [jax.ShapeDtypeStruct((8, 2, width // 8, width), BF16)]
    if first:
        out_shape = [sums, low, low] + out_shape
    out_shape += [half, half, sums] if last else [sums, sums]
    anywhere = pl.BlockSpec(memory_space=pl.ANY)
    in_specs = [anywhere] * (len(ahead) + 2)
    if first:
        in_specs[:2] = [whole((width,))] * 2
    held = [
        pltpu.VMEM((2, rows, width), BF16),
        pltpu.VMEM((2, rows, width), BF16),
        pltpu.VMEM((width, width), BF16),
        pltpu.VMEM((width, width), BF16),
        pltpu.VMEM((rows, width), F32),
        pltpu.VMEM((rows, width), F32),
        pltpu.VMEM((8, 2, width // 8, width), BF16),
        pltpu.SemaphoreType.DMA((16,)),
    ]
    if first:
        held += [
            pltpu.VMEM((rows, width), BF16),
            pltpu.VMEM((rows, width), BF16),
            pltpu.VMEM((width, width), BF16),
        ]
    if last:
        held.append(pltpu.VMEM((rows, width), BF16))
    return pl.pallas_call(
        functools.partial(feed_kernel, number, int(other), first, last),
        grid_spec=pltpu.PrefetchScalarGridSpec(
            num_scalar_prefetch=1,
            grid=(1,),
            in_specs=in_specs,
            out_specs=[anywhere] * len(out_shape),
            scratch_shapes=held,
        ),
        out_shape=out_shape,
        cost_estimate=cost(12 * rows * width * width, 16 * rows * width + 8 * width * width),
        name="feed",
    )(place, *ahead, w_in, w_down)


def middle_kernel(
    resid, gradient, grads, w_out, gain, grad_resid, branch_out, grad_attended, norm_grads
):
    _, scaled, rstd = normalize(resid[...], 1.0, 0.0)
    inner, gain_part, bias_part = normalize_back(gradient[...], scaled, rstd, row_of(gain))
    sums = jnp.concatenate([gain_part[None], bias_part[None]], axis=0)
    whole_grad = grads[...].astype(F32) + inner
    grad_resid[...] = whole_grad
    branch = whole_grad.astype(BF16)
    branch_out[...] = branch
    grad_attended[...] = dot(branch, w_out[...], ((1,), (1,))).astype(BF16)
    before = jnp.where(pl.program_id(0) == 0, 0.0, norm_grads[...])
    norm_grads[...] = jnp.where(pl.program_id(0) == 0, sums, before + sums)


def middle(resid, gradient, grads, w_out, gain):
    rows, width = resid.shape
    block = pl.BlockSpec((BLOCK, width), lambda j: (j, 0))
    return pl.pallas_call(
        middle_kernel,
        grid=(rows // BLOCK,),
        in_specs=[block] * 3 + [whole((width, width)), whole((width,))],
        out_specs=[block, block, block, whole((2, width))],
        out_shape=[
            jax.ShapeDtypeStruct((rows, width), F32),
            jax.ShapeDtypeStruct((rows, width), BF16),
            jax.ShapeDtypeStruct((rows, width), BF16),
            jax.ShapeDtypeStruct((2, width), F32),
        ],
        cost_estimate=cost(2 * rows * width * width, 18 * rows * width),
        name="middle",
    )(resid, gradient, grads, w_out, gain)


def weight_kernel(place, back, normed, attended, branch, mine, theirs):
    step = pl.program_id(0)
    core = place[0]

    def write(left, right):
        product = dot(left[...], right[...], ((0,), (0,))).astype(BF16)
        share = product.shape[0] // 4
        for half in range(2):
            for target, owner, here in ((mine, core, place[1]), (theirs, 1 - core, place[2])):
                high, low = step >> 1, step & 1
                even, odd = 4 * high + 2 * half + low, 4 * half + 2 * high + low
                at = ((1 - owner) * even + owner * odd) ^ here
                first = product[2 * half * share : (2 * half + 1) * share]
                second = product[(2 * half + 1) * share : (2 * half + 2) * share]
                target[at, :, :] = jnp.where(owner == 0, first, second)

    pl.when(step < 3)(lambda: write(back, normed))
    pl.when(step >= 3)(lambda: write(attended, branch))


def weight_grad(place, back, normed, attended, branch):
    _, rows, width = back.shape
    share = width // 4
    return pl.pallas_call(
        weight_kernel,
        grid_spec=pltpu.PrefetchScalarGridSpec(
            num_scalar_prefetch=1,
            grid=(4,),
            in_specs=[pl.BlockSpec((None, rows, width), lambda t, s: (jnp.minimum(t, 2), 0, 0))]
            + [whole((rows, width))] * 3,
            out_specs=[whole((8, share, width))] * 2,
        ),
        out_shape=[jax.ShapeDtypeStruct((8, share, width), BF16)] * 2,
        cost_estimate=cost(8 * rows * width * width, 20 * rows * width),
        name="weight_grad",
    )(place, back, normed, attended, branch)


def spread_kernel(place, *refs):
    pieces, (down, into) = refs[:4], refs[-2:]
    step = pl.program_id(0)
    rows = pieces[0].shape[2]
    odd = place[1 + step // 4] & 1
    parts = 2
    size = rows // parts
    for number, piece in enumerate(pieces):

        @pl.when(step // 2 == number)
        def _():
            def move(number, _):
                index, part = number // parts, number % parts
                source = pl.ds(pl.multiple_of(part * size, size), size)
                target = pl.ds(pl.multiple_of((index ^ odd) * rows + part * size, size), size)
                down[target, :] = piece[index, 0, source, :].astype(F32)
                into[target, :] = piece[index, 1, source, :].astype(F32)
                return 0

            lax.fori_loop(0, 2 * parts, move, 0)


def spread(place, square, units, pieces, so_far):
    _, _, rows, width = pieces[0].shape

    def taken(number):
        return pl.BlockSpec(
            (2, 2, rows, width), lambda t, s: (jnp.clip(t - 2 * number, 0, 1), 0, 0, 0)
        )

    def pair(t, s):
        return (t & 3) ^ (jnp.where(t < 4, s[1], s[2]) >> 1)

    def column(t, s):
        return 2 * square + (s[0] ^ (t >> 2))

    return pl.pallas_call(
        spread_kernel,
        grid_spec=pltpu.PrefetchScalarGridSpec(
            num_scalar_prefetch=1,
            grid=(8,),
            in_specs=[taken(number) for number in range(4)]
            + [pl.BlockSpec(memory_space=pl.ANY)] * len(so_far),
            out_specs=[
                pl.BlockSpec((2 * rows, width), lambda t, s: (4 * column(t, s) + pair(t, s), 0)),
                pl.BlockSpec((2 * rows, width), lambda t, s: (pair(t, s), column(t, s))),
            ],
        ),
        out_shape=[
            jax.ShapeDtypeStruct((units, width), F32),
            jax.ShapeDtypeStruct((width, units), F32),
        ],
        input_output_aliases={5: 0, 6: 1} if so_far else {},
        cost_estimate=cost(0, 24 * width * width),
        name="spread",
    )(place, *pieces, *so_far)


def last_kernel(place, back, weights, tokens, grad_resid, gain, theirs, mine, norm_grads):
    step = pl.program_id(0)
    gradient = dot(back[0], weights[0], ((1,), (1,)))
    gradient += dot(back[1], weights[1], ((1,), (1,)))
    gradient += dot(back[2], weights[2], ((1,), (1,)))
    _, scaled, rstd = normalize(tokens[...].astype(F32), 1.0, 0.0)
    inner, gain_part, bias_part = normalize_back(gradient, scaled, rstd, row_of(gain))
    sums = jnp.concatenate([gain_part[None], bias_part[None]], axis=0)
    result = grad_resid[...] + inner
    half = pl.num_programs(0) // 2

    @pl.when(step < half)
    def _():
        theirs[...] = result.astype(BF16)

    @pl.when(step >= half)
    def _():
        mine[...] = result

    before = jnp.where(step == 0, 0.0, norm_grads[...])
    norm_grads[...] = jnp.where(step == 0, sums, before + sums)


def last(place, back, weights, tokens, grad_resid, gain):
    rows, width = tokens.shape
    steps = rows // BLOCK
    half = steps // 2

    def turn(j, s):
        return (j + half * (1 - s[0])) % steps

    block = pl.BlockSpec((BLOCK, width), lambda j, s: (turn(j, s), 0))
    return pl.pallas_call(
        last_kernel,
        grid_spec=pltpu.PrefetchScalarGridSpec(
            num_scalar_prefetch=1,
            grid=(steps,),
            in_specs=[
                pl.BlockSpec((3, BLOCK, width), lambda j, s: (0, turn(j, s), 0)),
                whole((3, width, width)),
                block,
                block,
                whole((width,)),
            ],
            out_specs=[
                pl.BlockSpec((BLOCK, width), lambda j, s: (jnp.minimum(j, half - 1), 0)),
                pl.BlockSpec((BLOCK, width), lambda j, s: (jnp.maximum(j - half, 0), 0)),
                whole((2, width)),
            ],
        ),
        out_shape=[
            jax.ShapeDtypeStruct((rows // 2, width), BF16),
            jax.ShapeDtypeStruct((rows // 2, width), F32),
            jax.ShapeDtypeStruct((2, width), F32),
        ],
        cost_estimate=cost(6 * rows * width * width, 16 * rows * width + 6 * width * width),
        name="last",
    )(place, back, weights, tokens, grad_resid, gain)


def bit_of(axis, bit):
    return (lax.axis_index(axis) >> bit) & 1


def swap(values, axis, bit):
    count = lax.axis_size(axis)
    return lax.ppermute(values, axis, [(i, i ^ (1 << bit)) for i in range(count)])


class Stage:
    def __init__(self, dp_bits, even, odd):
        flips = [1 << (bit + 2 if axis == "dp" else bit) for axis, bit in (even, odd)]
        self.pairs = [(index, index ^ flips[index & 1]) for index in range(4 << dp_bits)]

    def send(self, values):
        return lax.ppermute(values, ("dp", "mp"), self.pairs)


class Sum:
    def __init__(self, terms, halving, adding, doubling):
        self.terms = terms
        self.count = terms[0].shape[0]
        self.halving, self.adding, self.doubling = list(halving), list(adding), list(doubling)
        self.pieces = None
        self.prepare()

    def total(self, low, high):
        result = None
        for term in self.terms:
            term = term[low:high].astype(F32)
            result = term if result is None else result + term
        return result.astype(BF16)

    def land(self, values):
        self.received = self.pieces[1] = values

    def prepare(self):
        if self.halving:
            self.outgoing = self.total(self.count // 2, self.count)
        elif self.terms:
            self.outgoing = self.total(0, self.count)

    def start(self):
        stage = (self.halving or self.adding or self.doubling)[0]
        self.received = stage.send(self.outgoing)

    def finish(self):
        if self.halving:
            self.halving.pop(0)
            self.count //= 2
            self.terms.append(self.received)
            self.prepare()
        elif self.adding:
            self.adding.pop(0)
            self.terms = [self.outgoing, self.received]
            self.prepare()
            if self.adding:
                self.start()
                self.finish()
        else:
            self.doubling.pop(0)
            self.terms = []
            self.pieces = [self.outgoing, self.received]
            if self.doubling:
                self.outgoing = jnp.concatenate(self.pieces, axis=0)


class Whole:
    def __init__(self, values, stages):
        self.outgoing, self.stages = values, list(stages)

    def start(self):
        self.received = self.stages.pop(0).send(self.outgoing)

    def finish(self):
        self.outgoing = self.outgoing + self.received


class Once:
    def __init__(self, values, stage):
        self.outgoing, self.stage = values, stage

    def start(self):
        self.received = self.stage.send(self.outgoing)

    def finish(self):
        pass

    def land(self, values):
        self.received = values


def local(
    dp_bits,
    tokens,
    segment_ids,
    norm1_gain,
    norm1_bias,
    w_qkv,
    conv_weight,
    w_out,
    norm2_gain,
    norm2_bias,
    w_in,
    w_down,
    cotangent,
):
    width = tokens.shape[2]
    core = bit_of("mp", 0)
    group = lax.axis_index("mp")
    rows = tokens.shape[1]

    def own_tokens(mine, theirs):
        at = lax.broadcasted_iota(jnp.int32, (2, 1, 1), 0)
        return jnp.where(at == core, mine[None], theirs.astype(mine.dtype)[None])

    dp = [("dp", bit) for bit in range(dp_bits)]
    y, cores = ("mp", 1), ("mp", 0)
    swap_cores = Stage(dp_bits, cores, cores)
    first, second = Stage(dp_bits, dp[0], y), Stage(dp_bits, y, dp[0])
    third = Stage(dp_bits, dp[1], dp[1])
    across = Stage(dp_bits, dp[0], dp[0])
    adding = [Stage(dp_bits, axis, axis) for axis in dp[2:]]
    x_bit, y_bit, z_bit = bit_of(*dp[0]), bit_of(*y), bit_of(*dp[1])
    here_even, here_odd = 4 * x_bit + 2 * y_bit + z_bit, 4 * y_bit + 2 * x_bit + z_bit
    here = jnp.where(core == 0, here_even, here_odd)
    here_theirs = jnp.where(core == 0, here_odd, here_even)
    place = jnp.stack([core, here, here_theirs, y_bit])

    their_tokens = swap(tokens, "mp", 0)
    taps_local, their_tokens = lax.optimization_barrier(
        (conv_weight.reshape(9, conv_weight.shape[2]), their_tokens)
    )
    their_cotangent = swap(cotangent, "mp", 0)
    pieces = [taps_local]
    for offset in range(1, 4):
        pieces.append(lax.ppermute(taps_local, "mp", [(i, i ^ offset) for i in range(4)]))
    stacked = jnp.stack(pieces, axis=0)
    taps = jnp.concatenate(
        [lax.dynamic_index_in_dim(stacked, group ^ i, 0, keepdims=False) for i in range(4)], axis=1
    )

    weights = w_qkv.transpose(1, 0, 2)
    so_far = front(place, tokens, norm1_gain, norm1_bias, weights, ())
    projected, normed_one, token_rows = front(
        place, their_tokens, norm1_gain, norm1_bias, weights, so_far
    )
    mixed, attended, lse, *masks = attend(place, projected, taps, segment_ids)
    masks = (taps, *masks)

    def feed_square(number, other, ahead):
        final = number == squares - 1 and not other
        return feed(number, other, final, place, ahead, w_in, w_down)

    squares = w_in.shape[1] // width // 2
    names = "abcdefgh"[:squares]
    found, units = {}, {}
    resid, normed_two, grad_output, other, *ahead = feed_square(
        0, True, (norm2_gain, norm2_bias, token_rows, attended, w_out, cotangent, their_cotangent)
    )
    units["core" + names[0]] = Once(other, swap_cores)

    def chunk_own(number):
        name = names[number]

        def run(ahead):
            own, *ahead = feed_square(number, False, (normed_two, *ahead, grad_output))
            units[name] = Sum(
                [own, units["core" + name].received], [first, second, third], adding, [third, second, first]
            )
            if number == squares - 1:
                theirs, found["output"], *ahead = ahead
                units["out"] = Once(theirs, swap_cores)
            return ahead

        return run

    def chunk_other(number):
        def run(ahead):
            other, *ahead = feed_square(number, True, (normed_two, *ahead, grad_output))
            units["core" + names[number]] = Once(other, swap_cores)
            return ahead

        return run

    def chunk_middle(ahead):
        back_sum = ahead[-1]
        grad_resid, branch, grad_attended, norm_two = middle(
            resid, back_sum, grad_output, w_out, norm2_gain
        )
        found.update(grad_resid=grad_resid, branch=branch, norm_two=norm_two, back=())
        return grad_attended

    def chunk_attend(first_pair, pairs):
        def run(held):
            grads = held[0] if isinstance(held, tuple) else held
            found["back"] = attend_back(
                first_pair, pairs, found["back"], mixed, grads, attended, lse, projected, *masks
            )
            found["grads"] = grads
            return (grads, found["back"][0])

        return run

    def chunk_weights(held):
        mine, theirs = weight_grad(place, held[1], normed_one, attended, found["branch"])
        found["mine"] = mine
        units["core"] = Once(theirs, swap_cores)
        return held[1]

    def chunk_last(back):
        theirs, found["input_grad"], found["norm_one"] = last(
            place, back, weights, token_rows, found["grad_resid"], norm1_gain
        )
        units["h"] = Sum(
            [found["mine"], units["core"].received], [first, second, third], adding, [third, across]
        )
        small = jnp.concatenate([found["back"][1], found["norm_one"], found["norm_two"]], axis=0)
        units["small"] = Whole(small, [Stage(dp_bits, axis, axis) for axis in [cores, y] + dp])
        units["in"] = Once(theirs, swap_cores)
        return found["input_grad"]

    def chunk_spread(square, name):
        def run(held):
            pieces = list(units[name].pieces) + [units[name + str(i)].received for i in range(2)]
            found["spread"] = spread(
                place, square, w_in.shape[1], pieces, found.get("spread", ())
            )
            return found["spread"]

        return run

    plan = [
        (("corea",), (), chunk_own(0)),
        (("a",), (), chunk_other(1)),
        (("a", "coreb"), (), chunk_own(1)),
        (("a", "b", "out"), (), chunk_middle),
        (("a", "b"), ("out",), chunk_attend(0, width // LANES // 2)),
        (("a", "b"), (), chunk_attend(width // LANES // 2, width // LANES // 2)),
        (("a", "b"), (), chunk_weights),
        (("core", "a", "b"), (), chunk_last),
        (("h", "a0", "in", "small"), ("a",), None),
        (("h", "a1", "small"), ("a0", "in"), None),
        (("h", "b", "small"), ("a1",), chunk_spread(0, "a")),
        (("h", "b", "small"), (), None),
        (("h", "b0", "b1", "small"), ("b",), None),
        (("h",), ("b0", "b1"), chunk_spread(1, "b")),
    ]
    held = ahead
    for sent, arrived, chunk in plan:
        for name in sent:
            if name not in units:
                units[name] = Once(units[name[0]].pieces[int(name[1])], swap_cores)
        active, landed = [units[name] for name in sent], [units[name] for name in arrived]
        outgoing, received, held = lax.optimization_barrier(
            (tuple(unit.outgoing for unit in active), tuple(unit.received for unit in landed), held)
        )
        for unit, values in zip(landed, received):
            unit.land(values)
        for unit, values in zip(active, outgoing):
            unit.outgoing = values
            unit.start()
        if chunk:
            held = chunk(held)
        for unit in active:
            unit.finish()

    small = units["small"]
    while small.stages:
        small.start()
        small.finish()
    share = width // 4
    small = lax.dynamic_slice_in_dim(small.outgoing, group * share, share, 1)
    heads = jnp.concatenate(units["h"].pieces, axis=0)
    heads = [
        lax.dynamic_index_in_dim(heads, index ^ (2 * x_bit + z_bit), 0, keepdims=False).astype(F32)
        for index in range(4)
    ]
    qkv_grad = jnp.stack(heads[:3]).transpose(2, 0, 1)
    out_grad = heads[3]
    down_grad, in_grad = found["spread"]
    return (
        own_tokens(found["output"], units["out"].received),
        own_tokens(found["input_grad"], units["in"].received),
        small[9],
        small[10],
        qkv_grad,
        small[:9].reshape(3, 3, share),
        out_grad,
        small[11],
        small[12],
        in_grad,
        down_grad,
    )


def solution(mesh):
    placed = (
        P(None, ("dp", "mp"), None),
        P(None, "dp"),
        P(),
        P(),
        P(),
        P(None, None, "mp"),
        P(),
        P(),
        P(),
        P(),
        P(),
        P(None, ("dp", "mp"), None),
    )
    dp_bits = mesh.shape["dp"].bit_length() - 1
    return jax.shard_map(
        functools.partial(local, dp_bits),
        mesh=mesh,
        in_specs=placed,
        out_specs=(
            P(None, ("dp", "mp"), None),
            P(None, ("dp", "mp"), None),
            P("mp"),
            P("mp"),
            P(None, None, "mp"),
            P(None, None, "mp"),
            P("mp", None),
            P("mp"),
            P("mp"),
            P(),
            P(),
        ),
        check_vma=False,
    )
```

profile of v0, /device:TPU:0, one launch (start us, length us, event | category | flops | bytes accessed | tf_op | source)
XLA Modules:
  0.0 311.6 jit_solution(7896467240881879272)
XLA Ops:
  2.6 6.8 %front.2 = (bf16[1024,2304]{1,0:T(8,128)(2,1)}, bf16[1024,768]{1,0:T(8,128)(2,1)}, bf16[1024,768]{1,0:T(8,128)(2,1)}) custom-call(s32[4]{0:T(128)} %pad_add_fusion.place, bf16[2,512,768]{2,1,0:T(8,128)(2,1)} %refs_0_.2, f32[768]{0:T(1024)} %gain.3, f32[768]{0:T(1024)} %refs_5_.5, bf16[3,768,768]{2,1,0:T(8,128)(2,1)} %bitcast.27), custom_call_target="tpu_custom_call" | custom-call | flops 1811939328 | bytes 9043968 | tf_op jit(solution)/shard_map/front/pallas_call | solution.py:303
  9.9 2.6 collective-permute-start.2
  12.5 6.8 %front.3 = (bf16[1024,2304]{1,0:T(8,128)(2,1)}, bf16[1024,768]{1,0:T(8,128)(2,1)}, bf16[1024,768]{1,0:T(8,128)(2,1)}) custom-call(s32[4]{0:T(128)} %pad_add_fusion.place, bf16[1024,2304]{1,0:T(8,128)(2,1)} %get-tuple-element.111.refs_0_, bf16[1024,768]{1,0:T(8,128)(2,1)} %get-tuple-element.112.refs_1_, ...), custom_call_target="tpu_custom_call", output_to_operand_aliasing={{0}: (1, {}), {1}: (2, {}), {2}: (3, {})} | custom-call | flops 1811939328 | bytes 9043968 | tf_op jit(solution)/shard_map/front/pallas_call | solution.py:303
  20.1 25.7 %attend.1 = (bf16[3,1024,768]{2,1,0:T(8,128)(2,1)}, bf16[1024,768]{1,0:T(8,128)(2,1)}, f32[6,2,1024]{2,1,0:T(2,128)}, f32[2,1024,128]{2,1,0:T(8,128)}, s32[1024,128]{1,0:T(8,128)}, /*index=5*/s32[8,1024]{1,0:T(8,128)}) custom-call(s32[4]{0:T(128)} %pad_add_fusion.place, ...), custom_call_target="tpu_custom_call" | custom-call | flops 3221225472 | bytes 12582912 | tf_op jit(solution)/shard_map/attend/pallas_call | solution.py:201
  47.0 18.6 %feed.4 = (f32[1024,768]{1,0:T(8,128)}, bf16[1024,768]{1,0:T(8,128)(2,1)}, bf16[1024,768]{1,0:T(8,128)(2,1)}, bf16[8,2,96,768]{3,2,1,0:T(8,128)(2,1)}, f32[1024,768]{1,0:T(8,128)}, /*index=5*/f32[1024,768]{1,0:T(8,128)}) custom-call(s32[4]{0:T(128)} %pad_add_fusion.place, f32[768]{0:T(1024)} %gain.2, f32[768]{0:T(1024)} %refs_1_.3, ...), custom_call_target="tpu_custom_call" | custom-call | flops 7247757312 | bytes 17301504 | tf_op jit(solution)/shard_map/feed/pallas_call | solution.py:481
  65.9 15.4 %feed.5 = (bf16[8,2,96,768]{3,2,1,0:T(8,128)(2,1)}, f32[1024,768]{1,0:T(8,128)}, f32[1024,768]{1,0:T(8,128)}) custom-call(s32[4]{0:T(128)} %pad_add_fusion.place, bf16[1024,768]{1,0:T(8,128)(2,1)} %get-tuple-element.119.refs_0_, f32[1024,768]{1,0:T(8,128)} %get-tuple-element.123.refs_1_, f32[1024,768]{1,0:T(8,128)} %get-tuple-element.124.refs_2_, ...), custom_call_target="tpu_custom_call" | custom-call | flops 7247757312 | bytes 17301504 | tf_op jit(solution)/shard_map/feed/pallas_call | solution.py:481
  81.3 2.4 add_convert_fusion.2
  83.7 2.0 collective-permute-start.6
  85.7 15.7 %feed.6 = (bf16[8,2,96,768]{3,2,1,0:T(8,128)(2,1)}, f32[1024,768]{1,0:T(8,128)}, f32[1024,768]{1,0:T(8,128)}) custom-call(s32[4]{0:T(128)} %pad_add_fusion.place, bf16[1024,768]{1,0:T(8,128)(2,1)} %get-tuple-element.119.refs_0_, f32[1024,768]{1,0:T(8,128)} %get-tuple-element.131.refs_1_, f32[1024,768]{1,0:T(8,128)} %get-tuple-element.132.refs_2_, ...), custom_call_target="tpu_custom_call" | custom-call | flops 7247757312 | bytes 17301504 | tf_op jit(solution)/shard_map/feed/pallas_call | solution.py:481
  101.4 1.5 add_convert_fusion.5
  102.9 1.6 collective-permute-start.7
  104.5 14.9 %feed.7 = (bf16[8,2,96,768]{3,2,1,0:T(8,128)(2,1)}, bf16[512,768]{1,0:T(8,128)(2,1)}, bf16[512,768]{1,0:T(8,128)(2,1)}, f32[1024,768]{1,0:T(8,128)}) custom-call(s32[4]{0:T(128)} %pad_add_fusion.place, bf16[1024,768]{1,0:T(8,128)(2,1)} %get-tuple-element.119.refs_0_, f32[1024,768]{1,0:T(8,128)} %get-tuple-element.136.refs_1_, ...), custom_call_target="tpu_custom_call" | custom-call | flops 7247757312 | bytes 17301504 | tf_op jit(solution)/shard_map/feed/pallas_call | solution.py:481
  119.5 2.2 add_convert_fusion.14
  121.7 1.5 add_convert_fusion.1
  124.0 1.6 collective-permute-start.9
  125.5 8.0 %middle.1 = (f32[1024,768]{1,0:T(8,128)}, bf16[1024,768]{1,0:T(8,128)(2,1)}, bf16[1024,768]{1,0:T(8,128)(2,1)}, f32[2,768]{1,0:T(2,128)}) custom-call(f32[1024,768]{1,0:T(8,128)} %get-tuple-element.147.resid, f32[1024,768]{1,0:T(8,128)} %get-tuple-element.148.gradient, bf16[1024,768]{1,0:T(8,128)(2,1)} %get-tuple-element.125.refs_3_.grads, ...), custom_call_target="tpu_custom_call" | custom-call | flops 1207959552 | bytes 14155776 | tf_op jit(solution)/shard_map/middle/pallas_call | solution.py:514
  133.5 2.2 add_convert_fusion.13
  135.7 3.9 %collective-permute-done.10 = bf16[4,2,96,768]{3,2,1,0:T(8,128)(2,1)} collective-permute-done((bf16[4,2,96,768]{3,2,1,0:T(8,128)(2,1)S(1)}, bf16[4,2,96,768]{3,2,1,0:T(8,128)(2,1)}, u32[]{:S(2)}, u32[]{:S(2)}) %collective-permute-start.10) | collective-permute-done | bytes 1179680 | tf_op jit(solution)/shard_map/ppermute | solution.py:701
  139.6 2.3 add_convert_fusion.4
  142.4 2.6 collective-permute-start.12
  145.0 18.8 %attend_back.2 = (bf16[3,1024,768]{2,1,0:T(8,128)(2,1)}, f32[9,768]{1,0:T(8,128)}) custom-call(bf16[3,1024,768]{2,1,0:T(8,128)(2,1)} %get-tuple-element.154.refs_0_.refs_2_, bf16[1024,768]{1,0:T(8,128)(2,1)} %get-tuple-element.162.refs_1_.refs_3_, bf16[1024,768]{1,0:T(8,128)(2,1)} %get-tuple-element.118.refs_3_.refs_2_.refs_4_.attended, ...), custom_call_target="tpu_custom_call" | custom-call | flops 4026531840 | bytes 8650752 | tf_op jit(solution)/shard_map/attend_back/pallas_call | solution.py:247
  166.0 1.6 collective-permute-start.15
  168.1 19.0 %attend_back.3 = (bf16[3,1024,768]{2,1,0:T(8,128)(2,1)}, f32[9,768]{1,0:T(8,128)}) custom-call(bf16[3,1024,768]{2,1,0:T(8,128)(2,1)} %get-tuple-element.159.refs_0_, f32[9,768]{1,0:T(8,128)} %get-tuple-element.163.refs_1_, bf16[3,1024,768]{2,1,0:T(8,128)(2,1)} %get-tuple-element.154.refs_0_.refs_2_, ...), custom_call_target="tpu_custom_call", output_to_operand_aliasing={{0}: (0, {}), {1}: (1, {})} | custom-call | flops 4026531840 | bytes 8650752 | tf_op jit(solution)/shard_map/attend_back/pallas_call | solution.py:247
  187.1 1.3 add_convert_fusion.10
  189.9 1.5 collective-permute-start.16
  191.4 11.5 %weight_grad.1 = (bf16[8,192,768]{2,1,0:T(8,128)(2,1)}, bf16[8,192,768]{2,1,0:T(8,128)(2,1)}) custom-call(s32[4]{0:T(128)} %pad_add_fusion.place, bf16[3,1024,768]{2,1,0:T(8,128)(2,1)} %get-tuple-element.171.back, bf16[1024,768]{1,0:T(8,128)(2,1)} %get-tuple-element.166.normed, bf16[1024,768]{1,0:T(8,128)(2,1)} %get-tuple-element.118.refs_3_.refs_2_.refs_4_.attended, ...), custom_call_target="tpu_custom_call" | custom-call | flops 4831838208 | bytes 15728640 | tf_op jit(solution)/shard_map/weight_grad/pallas_call | solution.py:553
  205.8 10.7 %last.1 = (bf16[512,768]{1,0:T(8,128)(2,1)}, f32[512,768]{1,0:T(8,128)}, f32[2,768]{1,0:T(2,128)}) custom-call(s32[4]{0:T(128)} %pad_add_fusion.place, bf16[3,1024,768]{2,1,0:T(8,128)(2,1)} %get-tuple-element.171.back, bf16[3,768,768]{2,1,0:T(8,128)(2,1)} %bitcast.29, bf16[1024,768]{1,0:T(8,128)(2,1)} %get-tuple-element.115.refs_2_.tokens, ...), custom_call_target="tpu_custom_call" | custom-call | flops 3623878656 | bytes 16121856 | tf_op jit(solution)/shard_map/last/pallas_call | solution.py:658
  217.4 1.6 add_convert_fusion
  219.0 2.1 collective-permute-done.19.refs_1_
  222.7 3.5 %collective-permute-done.21 = f32[13,768]{1,0:T(8,128)S(1)} collective-permute-done((f32[13,768]{1,0:T(8,128)S(1)}, f32[13,768]{1,0:T(8,128)S(1)}, u32[]{:S(2)}, u32[]{:S(2)}) %collective-permute-start.21) | collective-permute-done | bytes 39968 | tf_op jit(solution)/shard_map/ppermute | solution.py:701
  226.2 11.2 %collective-permute-done.20 = bf16[4,192,768]{2,1,0:T(8,128)(2,1)S(1)} collective-permute-done((bf16[4,192,768]{2,1,0:T(8,128)(2,1)S(1)}, bf16[4,192,768]{2,1,0:T(8,128)(2,1)S(1)}, u32[]{:S(2)}, u32[]{:S(2)}) %collective-permute-start.20) | collective-permute-done | bytes 1179680 | tf_op jit(solution)/shard_map/ppermute | solution.py:701
  237.4 1.7 add_convert_fusion.3
  239.2 1.6 collective-permute-start.24
  242.0 7.3 %collective-permute-done.25 = bf16[1,2,96,768]{3,2,1,0:T(8,128)(2,1)S(1)} collective-permute-done((bf16[1,2,96,768]{3,2,1,0:T(8,128)(2,1)S(1)}, bf16[1,2,96,768]{3,2,1,0:T(8,128)(2,1)S(1)}, u32[]{:S(2)}, u32[]{:S(2)}) %collective-permute-start.25) | collective-permute-done | bytes 294944 | tf_op jit(solution)/shard_map/ppermute | solution.py:701
  250.8 1.8 add_convert_fusion.8
  253.7 1.4 collective-permute-start.29
  256.1 9.1 %spread.2 = (f32[3072,768]{1,0:T(8,128)}, f32[768,3072]{1,0:T(8,128)}) custom-call(s32[4]{0:T(128)} %pad_add_fusion.place, bf16[4,2,96,768]{3,2,1,0:T(8,128)(2,1)} %copy-done.1, bf16[4,2,96,768]{3,2,1,0:T(8,128)(2,1)} %collective-permute-done.19.refs_1_, bf16[4,2,96,768]{3,2,1,0:T(8,128)(2,1)} %copy-done.7, bf16[4,2,96,768]{3,2,1,0:T(8,128)(2,1)} %copy-done.8), custom_call_target="tpu_custom_call" | custom-call | bytes 14155776 | tf_op jit(solution)/shard_map/spread/pallas_call | solution.py:604
  266.1 1.3 add_convert_fusion.7
  269.6 2.4 collective-permute-start.31
  272.5 4.5 %collective-permute-done.33 = f32[13,768]{1,0:T(8,128)S(1)} collective-permute-done((f32[13,768]{1,0:T(8,128)S(1)}, f32[13,768]{1,0:T(8,128)S(1)}, u32[]{:S(2)}, u32[]{:S(2)}) %collective-permute-start.33) | collective-permute-done | bytes 39968 | tf_op jit(solution)/shard_map/ppermute | solution.py:701
  277.0 6.5 %collective-permute-done.31 = bf16[1,192,768]{2,1,0:T(8,128)(2,1)S(1)} collective-permute-done((bf16[1,192,768]{2,1,0:T(8,128)(2,1)S(1)}, bf16[1,192,768]{2,1,0:T(8,128)(2,1)S(1)}, u32[]{:S(2)}, u32[]{:S(2)}) %collective-permute-start.31) | collective-permute-done | bytes 294944 | tf_op jit(solution)/shard_map/ppermute | solution.py:701
  285.4 1.7 collective-permute-start.35
  287.1 2.8 broadcast_select_fusion.1
  290.1 1.4 collective-permute-start.34
  291.4 4.0 %collective-permute-done.35 = bf16[1,192,768]{2,1,0:T(8,128)(2,1)S(1)} collective-permute-done((bf16[1,192,768]{2,1,0:T(8,128)(2,1)S(1)}, bf16[1,192,768]{2,1,0:T(8,128)(2,1)S(1)}, u32[]{:S(2)}, u32[]{:S(2)}) %collective-permute-start.35) | collective-permute-done | bytes 294944 | tf_op jit(solution)/shard_map/ppermute | solution.py:701
  296.8 1.9 broadcast_select_fusion
  300.0 9.2 %spread.3 = (f32[3072,768]{1,0:T(8,128)}, f32[768,3072]{1,0:T(8,128)}) custom-call(s32[4]{0:T(128)} %pad_add_fusion.place, bf16[4,2,96,768]{3,2,1,0:T(8,128)(2,1)} %copy-done, bf16[4,2,96,768]{3,2,1,0:T(8,128)(2,1)} %copy-done.6, bf16[4,2,96,768]{3,2,1,0:T(8,128)(2,1)} %collective-permute-done.36.refs_2_, ...), custom_call_target="tpu_custom_call", output_to_operand_aliasing={{0}: (5, {}), {1}: (6, {})} | custom-call | bytes 14155776 | tf_op jit(solution)/shard_map/spread/pallas_call | solution.py:604
  310.2 1.3 convert_bitcast_fusion
  (119 shorter events, 29.4 us)
Async XLA Ops:
  0.6 8.8 %collective-permute-start = (bf16[2,512,768]{2,1,0:T(8,128)(2,1)}, bf16[2,512,768]{2,1,0:T(8,128)(2,1)S(1)}, u32[]{:S(2)}, u32[]{:S(2)}) collective-permute-start(bf16[2,512,768]{2,1,0:T(8,128)(2,1)} %refs_0_.2), channel_id=1, source_target_pairs={{0,1},{1,0},{2,3},{3,2},{4,5},{5,4},{6,7},{7,6},{8,9},{9,8},{10,11... | collective-permute-start | bytes 4718600 | tf_op jit(solution)/shard_map/ppermute | solution.py:692
  1.2 44.6 %collective-permute-start.4 = (bf16[2,512,768]{2,1,0:T(8,128)(2,1)}, bf16[2,512,768]{2,1,0:T(8,128)(2,1)S(1)}, u32[]{:S(2)}, u32[]{:S(2)}) collective-permute-start(bf16[2,512,768]{2,1,0:T(8,128)(2,1)} %refs_5_.6), channel_id=1, source_target_pairs={{0,1},{1,0},{2,3},{3,2},{4,5},{5,4},{6,7},{7,6},{8,9},{9,8},{10,11... | collective-permute-start | bytes 4718600 | tf_op jit(solution)/shard_map/ppermute | solution.py:692
  9.4 9.9 %collective-permute-start.1 = (f32[9,192]{1,0:T(8,128)S(1)}, f32[9,192]{1,0:T(8,128)S(1)}, u32[]{:S(2)}, u32[]{:S(2)}) collective-permute-start(f32[9,192]{1,0:T(8,128)S(1)} %reshape.39), channel_id=1, source_target_pairs={{0,1},{1,0},{2,3},{3,2},{4,5},{5,4},{6,7},{7,6},{8,9},{9,8},{10,11... | collective-permute-start | bytes 20744 | tf_op jit(solution)/shard_map/ppermute | solution.py:822
  9.9 9.4 %collective-permute-start.2 = (f32[9,192]{1,0:T(8,128)S(1)}, f32[9,192]{1,0:T(8,128)S(1)}, u32[]{:S(2)}, u32[]{:S(2)}) collective-permute-start(f32[9,192]{1,0:T(8,128)S(1)} %reshape.39), channel_id=1, source_target_pairs={{0,2},{1,3},{2,0},{3,1},{4,6},{5,7},{6,4},{7,5},{8,10},{9,11},{10,... | collective-permute-start | bytes 20744 | tf_op jit(solution)/shard_map/ppermute | solution.py:822
  12.5 6.8 %collective-permute-start.3 = (f32[9,192]{1,0:T(8,128)S(1)}, f32[9,192]{1,0:T(8,128)S(1)}, u32[]{:S(2)}, u32[]{:S(2)}) collective-permute-start(f32[9,192]{1,0:T(8,128)S(1)} %reshape.39), channel_id=1, source_target_pairs={{0,3},{1,2},{2,1},{3,0},{4,7},{5,6},{6,5},{7,4},{8,11},{9,10},{10,... | collective-permute-start | bytes 20744 | tf_op jit(solution)/shard_map/ppermute | solution.py:822
  65.7 15.6 %collective-permute-start.5 = (bf16[8,2,96,768]{3,2,1,0:T(8,128)(2,1)}, bf16[8,2,96,768]{3,2,1,0:T(8,128)(2,1)S(1)}, u32[]{:S(2)}, u32[]{:S(2)}) collective-permute-start(bf16[8,2,96,768]{3,2,1,0:T(8,128)(2,1)} %get-tuple-element.127), channel_id=1, source_target_pairs={{0,1},{1,0},{2,3},{3,2},{4,5},{5,4},{6,7},{7,6},{8,9},{9,8},{10,11... | collective-permute-start | bytes 7077896 | tf_op jit(solution)/shard_map/ppermute | solution.py:701
  81.3 20.1 %copy-start.3 = (bf16[8,2,96,768]{3,2,1,0:T(8,128)(2,1)}, bf16[8,2,96,768]{3,2,1,0:T(8,128)(2,1)S(1)}, u32[]{:S(2)}) copy-start(bf16[8,2,96,768]{3,2,1,0:T(8,128)(2,1)S(1)} %collective-permute-done.5) | copy-start | bytes 7077892
  83.7 17.7 %collective-permute-start.6 = (bf16[4,2,96,768]{3,2,1,0:T(8,128)(2,1)S(1)}, bf16[4,2,96,768]{3,2,1,0:T(8,128)(2,1)}, u32[]{:S(2)}, u32[]{:S(2)}) collective-permute-start(bf16[4,2,96,768]{3,2,1,0:T(8,128)(2,1)S(1)} %add_convert_fusion.2), channel_id=1, source_target_pairs={{0,4},{1,3},{2,6},{3,1},{4,0},{5,7},{6,2},{7,5},{8,12},{9,11},{10,... | collective-permute-start | bytes 3538952 | tf_op jit(solution)/shard_map/ppermute | solution.py:701
  102.9 18.9 %collective-permute-start.8 = (bf16[8,2,96,768]{3,2,1,0:T(8,128)(2,1)}, bf16[8,2,96,768]{3,2,1,0:T(8,128)(2,1)S(1)}, u32[]{:S(2)}, u32[]{:S(2)}) collective-permute-start(bf16[8,2,96,768]{3,2,1,0:T(8,128)(2,1)} %get-tuple-element.141), channel_id=1, source_target_pairs={{0,1},{1,0},{2,3},{3,2},{4,5},{5,4},{6,7},{7,6},{8,9},{9,8},{10,11... | collective-permute-start | bytes 7077896 | tf_op jit(solution)/shard_map/ppermute | solution.py:701
  102.9 16.5 %collective-permute-start.7 = (bf16[2,2,96,768]{3,2,1,0:T(8,128)(2,1)S(1)}, bf16[2,2,96,768]{3,2,1,0:T(8,128)(2,1)S(1)}, u32[]{:S(2)}, u32[]{:S(2)}) collective-permute-start(bf16[2,2,96,768]{3,2,1,0:T(8,128)(2,1)S(1)} %add_convert_fusion.5), channel_id=1, source_target_pairs={{0,2},{1,5},{2,0},{3,7},{4,6},{5,1},{6,4},{7,3},{8,10},{9,13},{10,... | collective-permute-start | bytes 1769480 | tf_op jit(solution)/shard_map/ppermute | solution.py:701
  123.3 16.4 %collective-permute-start.10 = (bf16[4,2,96,768]{3,2,1,0:T(8,128)(2,1)S(1)}, bf16[4,2,96,768]{3,2,1,0:T(8,128)(2,1)}, u32[]{:S(2)}, u32[]{:S(2)}) collective-permute-start(bf16[4,2,96,768]{3,2,1,0:T(8,128)(2,1)S(1)} %add_convert_fusion.1), channel_id=1, source_target_pairs={{0,4},{1,3},{2,6},{3,1},{4,0},{5,7},{6,2},{7,5},{8,12},{9,11},{10,... | collective-permute-start | bytes 3538952 | tf_op jit(solution)/shard_map/ppermute | solution.py:701
  124.0 9.5 %collective-permute-start.9 = (bf16[1,2,96,768]{3,2,1,0:T(8,128)(2,1)}, bf16[1,2,96,768]{3,2,1,0:T(8,128)(2,1)}, u32[]{:S(2)}, u32[]{:S(2)}) collective-permute-start(bf16[1,2,96,768]{3,2,1,0:T(8,128)(2,1)} %add_convert_fusion.14), channel_id=1, source_target_pairs={{0,8},{1,9},{2,10},{3,11},{4,12},{5,13},{6,14},{7,15},{8,0},{9,1},... | collective-permute-start | bytes 884744 | tf_op jit(solution)/shard_map/ppermute | solution.py:701
  125.5 16.4 %collective-permute-start.11 = (bf16[512,768]{1,0:T(8,128)(2,1)}, bf16[512,768]{1,0:T(8,128)(2,1)}, u32[]{:S(2)}, u32[]{:S(2)}) collective-permute-start(bf16[512,768]{1,0:T(8,128)(2,1)} %get-tuple-element.146), channel_id=1, source_target_pairs={{0,1},{1,0},{2,3},{3,2},{4,5},{5,4},{6,7},{7,6},{8,9},{9,8},{10,11... | collective-permute-start | bytes 2359304 | tf_op jit(solution)/shard_map/ppermute | solution.py:701
  141.9 22.9 %collective-permute-start.13 = (bf16[2,2,96,768]{3,2,1,0:T(8,128)(2,1)}, bf16[2,2,96,768]{3,2,1,0:T(8,128)(2,1)S(1)}, u32[]{:S(2)}, u32[]{:S(2)}) collective-permute-start(bf16[2,2,96,768]{3,2,1,0:T(8,128)(2,1)} %add_convert_fusion.4), channel_id=1, source_target_pairs={{0,2},{1,5},{2,0},{3,7},{4,6},{5,1},{6,4},{7,3},{8,10},{9,13},{10,... | collective-permute-start | bytes 1769480 | tf_op jit(solution)/shard_map/ppermute | solution.py:701
  142.4 21.4 %collective-permute-start.12 = (bf16[1,2,96,768]{3,2,1,0:T(8,128)(2,1)}, bf16[1,2,96,768]{3,2,1,0:T(8,128)(2,1)S(1)}, u32[]{:S(2)}, u32[]{:S(2)}) collective-permute-start(bf16[1,2,96,768]{3,2,1,0:T(8,128)(2,1)} %add_convert_fusion.13), channel_id=1, source_target_pairs={{0,16},{1,17},{2,18},{3,19},{4,20},{5,21},{6,22},{7,23},{8,24},{9,... | collective-permute-start | bytes 884744 | tf_op jit(solution)/shard_map/ppermute | solution.py:701
  166.0 21.1 %collective-permute-start.15 = (bf16[1,2,96,768]{3,2,1,0:T(8,128)(2,1)S(1)}, bf16[1,2,96,768]{3,2,1,0:T(8,128)(2,1)}, u32[]{:S(2)}, u32[]{:S(2)}) collective-permute-start(bf16[1,2,96,768]{3,2,1,0:T(8,128)(2,1)S(1)} %add_convert_fusion.11), channel_id=1, source_target_pairs={{0,8},{1,9},{2,10},{3,11},{4,12},{5,13},{6,14},{7,15},{8,0},{9,1},... | collective-permute-start | bytes 884744 | tf_op jit(solution)/shard_map/ppermute | solution.py:701
  167.7 20.8 %collective-permute-start.14 = (bf16[1,2,96,768]{3,2,1,0:T(8,128)(2,1)S(1)}, bf16[1,2,96,768]{3,2,1,0:T(8,128)(2,1)}, u32[]{:S(2)}, u32[]{:S(2)}) collective-permute-start(bf16[1,2,96,768]{3,2,1,0:T(8,128)(2,1)S(1)} %add_convert_fusion.12), channel_id=1, source_target_pairs={{0,8},{1,9},{2,10},{3,11},{4,12},{5,13},{6,14},{7,15},{8,0},{9,1},... | collective-permute-start | bytes 884744 | tf_op jit(solution)/shard_map/ppermute | solution.py:701
  189.5 14.3 %collective-permute-start.17 = (bf16[1,2,96,768]{3,2,1,0:T(8,128)(2,1)S(1)}, bf16[1,2,96,768]{3,2,1,0:T(8,128)(2,1)S(1)}, u32[]{:S(2)}, u32[]{:S(2)}) collective-permute-start(bf16[1,2,96,768]{3,2,1,0:T(8,128)(2,1)S(1)} %add_convert_fusion.10), channel_id=1, source_target_pairs={{0,16},{1,17},{2,18},{3,19},{4,20},{5,21},{6,22},{7,23},{8,24},{9,... | collective-permute-start | bytes 884744 | tf_op jit(solution)/shard_map/ppermute | solution.py:701
  189.9 14.7 %collective-permute-start.16 = (bf16[2,2,96,768]{3,2,1,0:T(8,128)(2,1)S(1)}, bf16[2,2,96,768]{3,2,1,0:T(8,128)(2,1)S(1)}, u32[]{:S(2)}, u32[]{:S(2)}) collective-permute-start(bf16[2,2,96,768]{3,2,1,0:T(8,128)(2,1)S(1)} %pad_maximum_fusion.2), channel_id=1, source_target_pairs={{0,2},{1,5},{2,0},{3,7},{4,6},{5,1},{6,4},{7,3},{8,10},{9,13},{10,... | collective-permute-start | bytes 1769480 | tf_op jit(solution)/shard_map/ppermute | solution.py:701
  204.7 17.4 %copy-start.1 = (bf16[4,2,96,768]{3,2,1,0:T(8,128)(2,1)}, bf16[4,2,96,768]{3,2,1,0:T(8,128)(2,1)S(1)}, u32[]{:S(2)}) copy-start(bf16[4,2,96,768]{3,2,1,0:T(8,128)(2,1)S(1)} %pad_maximum_fusion.refs_0_) | copy-start | bytes 3538948
  204.7 12.7 %collective-permute-start.18 = (bf16[8,192,768]{2,1,0:T(8,128)(2,1)}, bf16[8,192,768]{2,1,0:T(8,128)(2,1)}, u32[]{:S(2)}, u32[]{:S(2)}) collective-permute-start(bf16[8,192,768]{2,1,0:T(8,128)(2,1)} %get-tuple-element.175), channel_id=1, source_target_pairs={{0,1},{1,0},{2,3},{3,2},{4,5},{5,4},{6,7},{7,6},{8,9},{9,8},{10,11... | collective-permute-start | bytes 7077896 | tf_op jit(solution)/shard_map/ppermute | solution.py:701
  204.8 16.4 %collective-permute-start.19 = (bf16[4,2,96,768]{3,2,1,0:T(8,128)(2,1)S(1)}, bf16[4,2,96,768]{3,2,1,0:T(8,128)(2,1)}, u32[]{:S(2)}, u32[]{:S(2)}) collective-permute-start(bf16[4,2,96,768]{3,2,1,0:T(8,128)(2,1)S(1)} %pad_maximum_fusion.refs_0_), channel_id=1, source_target_pairs={{0,4},{1,3},{2,6},{3,1},{4,0},{5,7},{6,2},{7,5},{8,12},{9,11},{10,... | collective-permute-start | bytes 3538952 | tf_op jit(solution)/shard_map/ppermute | solution.py:701
  205.8 10.7 %copy-start.14 = (f32[2,768]{1,0:T(2,128)S(1)}, f32[2,768]{1,0:T(2,128)}, u32[]{:S(2)}) copy-start(f32[2,768]{1,0:T(2,128)} %get-tuple-element.180) | copy-start | bytes 18436
  205.8 11.6 %copy-start.2 = (bf16[8,192,768]{2,1,0:T(8,128)(2,1)S(1)}, bf16[8,192,768]{2,1,0:T(8,128)(2,1)}, u32[]{:S(2)}) copy-start(bf16[8,192,768]{2,1,0:T(8,128)(2,1)} %get-tuple-element.174) | copy-start | bytes 7077892
  219.0 21.8 %copy-start.9 = (bf16[1,2,96,768]{3,2,1,0:T(8,128)(2,1)S(1)}, bf16[1,2,96,768]{3,2,1,0:T(8,128)(2,1)}, u32[]{:S(2)}) copy-start(bf16[1,2,96,768]{3,2,1,0:T(8,128)(2,1)} %add_convert_fusion.9) | copy-start | bytes 884740
  221.2 16.2 %collective-permute-start.20 = (bf16[4,192,768]{2,1,0:T(8,128)(2,1)S(1)}, bf16[4,192,768]{2,1,0:T(8,128)(2,1)S(1)}, u32[]{:S(2)}, u32[]{:S(2)}) collective-permute-start(bf16[4,192,768]{2,1,0:T(8,128)(2,1)S(1)} %add_convert_fusion), channel_id=1, source_target_pairs={{0,4},{1,3},{2,6},{3,1},{4,0},{5,7},{6,2},{7,5},{8,12},{9,11},{10,... | collective-permute-start | bytes 3538952 | tf_op jit(solution)/shard_map/ppermute | solution.py:701
  222.1 16.9 %collective-permute-start.22 = (bf16[4,2,96,768]{3,2,1,0:T(8,128)(2,1)S(1)}, bf16[4,2,96,768]{3,2,1,0:T(8,128)(2,1)S(1)}, u32[]{:S(2)}, u32[]{:S(2)}) collective-permute-start(bf16[4,2,96,768]{3,2,1,0:T(8,128)(2,1)S(1)} %pad_maximum_fusion.refs_0_), channel_id=1, source_target_pairs={{0,1},{1,0},{2,3},{3,2},{4,5},{5,4},{6,7},{7,6},{8,9},{9,8},{10,11... | collective-permute-start | bytes 3538952 | tf_op jit(solution)/shard_map/ppermute | solution.py:701
  222.1 16.9 %collective-permute-start.23 = (bf16[512,768]{1,0:T(8,128)(2,1)S(1)}, bf16[512,768]{1,0:T(8,128)(2,1)S(1)}, u32[]{:S(2)}, u32[]{:S(2)}) collective-permute-start(bf16[512,768]{1,0:T(8,128)(2,1)S(1)} %copy-done.16), channel_id=1, source_target_pairs={{0,1},{1,0},{2,3},{3,2},{4,5},{5,4},{6,7},{7,6},{8,9},{9,8},{10,11... | collective-permute-start | bytes 2359304 | tf_op jit(solution)/shard_map/ppermute | solution.py:701
  222.7 3.5 %collective-permute-start.21 = (f32[13,768]{1,0:T(8,128)S(1)}, f32[13,768]{1,0:T(8,128)S(1)}, u32[]{:S(2)}, u32[]{:S(2)}) collective-permute-start(f32[13,768]{1,0:T(8,128)S(1)} %pad_maximum_fusion.7), channel_id=1, source_target_pairs={{0,1},{1,0},{2,3},{3,2},{4,5},{5,4},{6,7},{7,6},{8,9},{9,8},{10,11... | collective-permute-start | bytes 119816 | tf_op jit(solution)/shard_map/ppermute | solution.py:701
  237.4 13.4 %copy-start.10 = (bf16[4,192,768]{2,1,0:T(8,128)(2,1)}, bf16[4,192,768]{2,1,0:T(8,128)(2,1)S(1)}, u32[]{:S(2)}) copy-start(bf16[4,192,768]{2,1,0:T(8,128)(2,1)S(1)} %collective-permute-done.20) | copy-start | bytes 3538948
  239.1 16.0 %copy-start.11 = (bf16[512,768]{1,0:T(8,128)(2,1)}, bf16[512,768]{1,0:T(8,128)(2,1)S(1)}, u32[]{:S(2)}) copy-start(bf16[512,768]{1,0:T(8,128)(2,1)S(1)} %collective-permute-done.23) | copy-start | bytes 2359300
  239.1 13.5 %copy-start.7 = (bf16[4,2,96,768]{3,2,1,0:T(8,128)(2,1)}, bf16[4,2,96,768]{3,2,1,0:T(8,128)(2,1)S(1)}, u32[]{:S(2)}) copy-start(bf16[4,2,96,768]{3,2,1,0:T(8,128)(2,1)S(1)} %collective-permute-done.22.refs_2_) | copy-start | bytes 3538948
  239.1 13.5 %collective-permute-start.27 = (bf16[4,2,96,768]{3,2,1,0:T(8,128)(2,1)}, bf16[4,2,96,768]{3,2,1,0:T(8,128)(2,1)S(1)}, u32[]{:S(2)}, u32[]{:S(2)}) collective-permute-start(bf16[4,2,96,768]{3,2,1,0:T(8,128)(2,1)} %collective-permute-done.19.refs_1_), channel_id=1, source_target_pairs={{0,1},{1,0},{2,3},{3,2},{4,5},{5,4},{6,7},{7,6},{8,9},{9,8},{10,11... | collective-permute-start | bytes 3538952 | tf_op jit(solution)/shard_map/ppermute | solution.py:701
  239.2 11.6 %collective-permute-start.24 = (bf16[2,192,768]{2,1,0:T(8,128)(2,1)S(1)}, bf16[2,192,768]{2,1,0:T(8,128)(2,1)S(1)}, u32[]{:S(2)}, u32[]{:S(2)}) collective-permute-start(bf16[2,192,768]{2,1,0:T(8,128)(2,1)S(1)} %add_convert_fusion.3), channel_id=1, source_target_pairs={{0,2},{1,5},{2,0},{3,7},{4,6},{5,1},{6,4},{7,3},{8,10},{9,13},{10,... | collective-permute-start | bytes 1769480 | tf_op jit(solution)/shard_map/ppermute | solution.py:701
  240.8 8.5 %collective-permute-start.25 = (bf16[1,2,96,768]{3,2,1,0:T(8,128)(2,1)S(1)}, bf16[1,2,96,768]{3,2,1,0:T(8,128)(2,1)S(1)}, u32[]{:S(2)}, u32[]{:S(2)}) collective-permute-start(bf16[1,2,96,768]{3,2,1,0:T(8,128)(2,1)S(1)} %copy-done.9), channel_id=1, source_target_pairs={{0,8},{1,9},{2,10},{3,11},{4,12},{5,13},{6,14},{7,15},{8,0},{9,1},... | collective-permute-start | bytes 884744 | tf_op jit(solution)/shard_map/ppermute | solution.py:701
  240.8 9.4 %collective-permute-start.26 = (f32[13,768]{1,0:T(8,128)S(1)}, f32[13,768]{1,0:T(8,128)S(1)}, u32[]{:S(2)}, u32[]{:S(2)}) collective-permute-start(f32[13,768]{1,0:T(8,128)S(1)} %add.194), channel_id=1, source_target_pairs={{0,2},{1,3},{2,0},{3,1},{4,6},{5,7},{6,4},{7,5},{8,10},{9,11},{10,... | collective-permute-start | bytes 119816 | tf_op jit(solution)/shard_map/ppermute | solution.py:701
  253.7 13.8 %collective-permute-start.29 = (bf16[2,2,96,768]{3,2,1,0:T(8,128)(2,1)S(1)}, bf16[2,2,96,768]{3,2,1,0:T(8,128)(2,1)}, u32[]{:S(2)}, u32[]{:S(2)}) collective-permute-start(bf16[2,2,96,768]{3,2,1,0:T(8,128)(2,1)S(1)} %pad_maximum_fusion.3), channel_id=1, source_target_pairs={{0,2},{1,5},{2,0},{3,7},{4,6},{5,1},{6,4},{7,3},{8,10},{9,13},{10,... | collective-permute-start | bytes 1769480 | tf_op jit(solution)/shard_map/ppermute | solution.py:701
  255.0 11.1 %collective-permute-start.28 = (bf16[1,192,768]{2,1,0:T(8,128)(2,1)}, bf16[1,192,768]{2,1,0:T(8,128)(2,1)}, u32[]{:S(2)}, u32[]{:S(2)}) collective-permute-start(bf16[1,192,768]{2,1,0:T(8,128)(2,1)} %add_convert_fusion.8), channel_id=1, source_target_pairs={{0,8},{1,9},{2,10},{3,11},{4,12},{5,13},{6,14},{7,15},{8,0},{9,1},... | collective-permute-start | bytes 884744 | tf_op jit(solution)/shard_map/ppermute | solution.py:701
  255.0 10.2 %collective-permute-start.30 = (f32[13,768]{1,0:T(8,128)}, f32[13,768]{1,0:T(8,128)}, u32[]{:S(2)}, u32[]{:S(2)}) collective-permute-start(f32[13,768]{1,0:T(8,128)} %add.201), channel_id=1, source_target_pairs={{0,4},{1,5},{2,6},{3,7},{4,0},{5,1},{6,2},{7,3},{8,12},{9,13},{10,... | collective-permute-start | bytes 119816 | tf_op jit(solution)/shard_map/ppermute | solution.py:701
  268.6 21.3 %copy-start = (bf16[4,2,96,768]{3,2,1,0:T(8,128)(2,1)}, bf16[4,2,96,768]{3,2,1,0:T(8,128)(2,1)S(1)}, u32[]{:S(2)}) copy-start(bf16[4,2,96,768]{3,2,1,0:T(8,128)(2,1)S(1)} %pad_maximum_fusion.1.refs_0_) | copy-start | bytes 3538948
  268.6 16.3 %collective-permute-start.32 = (bf16[4,2,96,768]{3,2,1,0:T(8,128)(2,1)S(1)}, bf16[4,2,96,768]{3,2,1,0:T(8,128)(2,1)S(1)}, u32[]{:S(2)}, u32[]{:S(2)}) collective-permute-start(bf16[4,2,96,768]{3,2,1,0:T(8,128)(2,1)S(1)} %pad_maximum_fusion.1.refs_0_), channel_id=1, source_target_pairs={{0,4},{1,3},{2,6},{3,1},{4,0},{5,7},{6,2},{7,5},{8,12},{9,11},{10,... | collective-permute-start | bytes 3538952 | tf_op jit(solution)/shard_map/ppermute | solution.py:701
  269.6 13.9 %collective-permute-start.31 = (bf16[1,192,768]{2,1,0:T(8,128)(2,1)S(1)}, bf16[1,192,768]{2,1,0:T(8,128)(2,1)S(1)}, u32[]{:S(2)}, u32[]{:S(2)}) collective-permute-start(bf16[1,192,768]{2,1,0:T(8,128)(2,1)S(1)} %add_convert_fusion.7), channel_id=1, source_target_pairs={{0,16},{1,17},{2,18},{3,19},{4,20},{5,21},{6,22},{7,23},{8,24},{9,... | collective-permute-start | bytes 884744 | tf_op jit(solution)/shard_map/ppermute | solution.py:701
  272.0 4.9 %collective-permute-start.33 = (f32[13,768]{1,0:T(8,128)S(1)}, f32[13,768]{1,0:T(8,128)S(1)}, u32[]{:S(2)}, u32[]{:S(2)}) collective-permute-start(f32[13,768]{1,0:T(8,128)S(1)} %add.203), channel_id=1, source_target_pairs={{0,8},{1,9},{2,10},{3,11},{4,12},{5,13},{6,14},{7,15},{8,0},{9,1},... | collective-permute-start | bytes 119816 | tf_op jit(solution)/shard_map/ppermute | solution.py:701
  284.9 10.6 %collective-permute-start.36 = (bf16[4,2,96,768]{3,2,1,0:T(8,128)(2,1)S(1)}, bf16[4,2,96,768]{3,2,1,0:T(8,128)(2,1)}, u32[]{:S(2)}, u32[]{:S(2)}) collective-permute-start(bf16[4,2,96,768]{3,2,1,0:T(8,128)(2,1)S(1)} %pad_maximum_fusion.1.refs_0_), channel_id=1, source_target_pairs={{0,1},{1,0},{2,3},{3,2},{4,5},{5,4},{6,7},{7,6},{8,9},{9,8},{10,11... | collective-permute-start | bytes 3538952 | tf_op jit(solution)/shard_map/ppermute | solution.py:701
  284.9 10.6 %collective-permute-start.37 = (bf16[4,2,96,768]{3,2,1,0:T(8,128)(2,1)S(1)}, bf16[4,2,96,768]{3,2,1,0:T(8,128)(2,1)}, u32[]{:S(2)}, u32[]{:S(2)}) collective-permute-start(bf16[4,2,96,768]{3,2,1,0:T(8,128)(2,1)S(1)} %collective-permute-done.32.refs_1_), channel_id=1, source_target_pairs={{0,1},{1,0},{2,3},{3,2},{4,5},{5,4},{6,7},{7,6},{8,9},{9,8},{10,11... | collective-permute-start | bytes 3538952 | tf_op jit(solution)/shard_map/ppermute | solution.py:701
  285.4 10.0 %collective-permute-start.35 = (bf16[1,192,768]{2,1,0:T(8,128)(2,1)S(1)}, bf16[1,192,768]{2,1,0:T(8,128)(2,1)S(1)}, u32[]{:S(2)}, u32[]{:S(2)}) collective-permute-start(bf16[1,192,768]{2,1,0:T(8,128)(2,1)S(1)} %add_convert_fusion.6), channel_id=1, source_target_pairs={{0,8},{1,9},{2,10},{3,11},{4,12},{5,13},{6,14},{7,15},{8,0},{9,1},... | collective-permute-start | bytes 884744 | tf_op jit(solution)/shard_map/ppermute | solution.py:701
  290.1 8.7 %collective-permute-start.34 = (f32[13,768]{1,0:T(8,128)S(1)}, f32[13,768]{1,0:T(8,128)S(1)}, u32[]{:S(2)}, u32[]{:S(2)}) collective-permute-start(f32[13,768]{1,0:T(8,128)S(1)} %add.205), channel_id=1, source_target_pairs={{0,16},{1,17},{2,18},{3,19},{4,20},{5,21},{6,22},{7,23},{8,24},{9,... | collective-permute-start | bytes 119816 | tf_op jit(solution)/shard_map/ppermute | solution.py:701
  295.5 13.7 %collective-permute-start.38 = (bf16[2,192,768]{2,1,0:T(8,128)(2,1)S(1)}, bf16[2,192,768]{2,1,0:T(8,128)(2,1)S(1)}, u32[]{:S(2)}, u32[]{:S(2)}) collective-permute-start(bf16[2,192,768]{2,1,0:T(8,128)(2,1)S(1)} %pad_maximum_fusion.4), channel_id=1, source_target_pairs={{0,4},{1,5},{2,6},{3,7},{4,0},{5,1},{6,2},{7,3},{8,12},{9,13},{10,... | collective-permute-start | bytes 1769480 | tf_op jit(solution)/shard_map/ppermute | solution.py:701
  (8 other events, 27.0 us)
where the time goes:
time: 313 us; the launch traced here: 312 us
  Pallas kernels  190 us (61%)
  waiting for transfers between devices  46.2 us (15%)
  other arithmetic  36.2 us (12%)
  starting transfers between devices  33.7 us (11%)
  local copies, waits for them, and re-layouts  4.27 us (1%)
    pallas_call x4, Pallas kernels, feed(): pl.pallas_call(functools.partial(feed_kernel, number, int(other), first,...  64.6 us
    ppermute x34, waiting for transfers between devices, send(): return lax.ppermute(values, ('dp', 'mp'), self.pairs)  46.2 us
    pallas_call x2, Pallas kernels, attend_back(): pl.pallas_call(functools.partial(attend_back_kernel, bool(so_far)), grid=...  37.7 us
    ppermute x34, starting transfers between devices, send(): return lax.ppermute(values, ('dp', 'mp'), self.pairs)  29.9 us
    pallas_call x1, Pallas kernels, attend(): pl.pallas_call(attend_kernel, grid_spec=pltpu.PrefetchScalarGridSpec(num_...  25.7 us
    convert_element_type x15, other arithmetic, total(): return result.astype(BF16)  23 us
    pallas_call x2, Pallas kernels, spread(): pl.pallas_call(spread_kernel, grid_spec=pltpu.PrefetchScalarGridSpec(num_...  18.3 us
    pallas_call x2, Pallas kernels, front(): pl.pallas_call(functools.partial(front_kernel, bool(so_far)), grid_spec=p...  13.6 us
  transfers between devices with their start and end apart: 39, of which 11 were waited for; matrix products, arithmetic and copies ran while one was open for 9% of the time, Pallas kernels for 55%

commit v1 on v0

--- a/solution.py
+++ b/solution.py
@@ -342,7 +342,7 @@
         else:
             parts_out, out, back_out = refs[6:9]
             scratch = refs[9:]
-    lefts, rights, in_block, down_block, total, back, parts, sems = scratch
+    lefts, rights, in_block, down_block, total, back, parts, sems, row_sems = scratch
     hidden, normed, grads, grad_pre = lefts.at[0], lefts.at[1], rights.at[0], rights.at[1]
     count = normed.shape[0]
     width = in_block.shape[1]
@@ -360,20 +360,21 @@
 
     if first:
         early = [copy(attended, attended_held), copy(w_out, weights_held), copy(tokens, tokens_held)]
-        later = [copy(w_in.at[:, columns], in_block)]
-        last_in = [
+        for flight in early:
+            flight.wait()
+        later = [
+            copy(w_in.at[:, columns], in_block),
             copy(mine.at[core], grads.at[my_rows, :]),
             copy(theirs.at[core], grads.at[their_rows, :]),
             copy(w_down.at[columns, :], down_block),
         ]
     else:
-        early = [copy(normed_in, normed)]
-        later = [copy(w_in.at[:, columns], in_block)]
-        last_in = [copy(grads_in, grads), copy(w_down.at[columns, :], down_block)]
-        total_in = copy(out_in, total)
-        back_so_far = copy(back_in, back)
-    for flight in early:
-        flight.wait()
+        later = [
+            copy(normed_in, normed),
+            copy(w_in.at[:, columns], in_block),
+            copy(grads_in, grads),
+            copy(w_down.at[columns, :], down_block),
+        ]
     writes = []
     if first:
 
@@ -389,8 +390,11 @@
         lax.fori_loop(0, count // BLOCK, begin, 0)
         resid_flight = copy(total, resid_out)
         writes.append(copy(normed, normed_out))
-    for flight in later + last_in:
+    for flight in later:
         flight.wait()
+    if not first:
+        total_in = copy(out_in, total)
+        back_so_far = copy(back_in, back)
     if first:
         writes.append(copy(grads, grads_out))
     size = FEED_ROWS
@@ -423,6 +427,13 @@
     else:
         total_in.wait()
         back_so_far.wait()
+
+    def row_copies(step):
+        at = pl.ds(pl.multiple_of(step * size, size), size)
+        flights = [pltpu.make_async_copy(back.at[at, :], back_out.at[at, :], row_sems.at[0, step])]
+        if not last:
+            flights.append(pltpu.make_async_copy(total.at[at, :], out.at[at, :], row_sems.at[1, step]))
+        return flights
 
     def outer(step, _):
         at = pl.ds(pl.multiple_of(step * size, size), size)
@@ -433,15 +444,17 @@
             total[at, :] = value
         product = dot(grad_pre[at, :], in_block[...], ((1,), (1,)))
         back[at, :] = product if first else back[at, :] + product
+        for flight in row_copies(step):
+            flight.start()
         return 0
 
     lax.fori_loop(0, count // size, outer, 0)
     if last:
         writes.append(copy(result_low.at[their_rows, :], out_theirs))
         writes.append(copy(result_low.at[my_rows, :], out_mine))
-    else:
-        writes.append(copy(total, out))
-    writes.append(copy(back, back_out))
+    for step in range(count // size):
+        for flight in row_copies(step):
+            flight.wait()
     for flight in writes:
         flight.wait()
 
@@ -469,6 +482,7 @@
         pltpu.VMEM((rows, width), F32),
         pltpu.VMEM((8, 2, width // 8, width), BF16),
         pltpu.SemaphoreType.DMA((16,)),
+        pltpu.SemaphoreType.DMA((2, rows // FEED_ROWS)),
     ]
     if first:
         held += [
@@ -710,6 +724,8 @@
         self.prepare()
 
     def total(self, low, high):
+        if len(self.terms) == 2:
+            return self.terms[0][low:high] + self.terms[1][low:high]
         result = None
         for term in self.terms:
             term = term[low:high].astype(F32)
@@ -830,6 +846,7 @@
     projected, normed_one, token_rows = front(
         place, their_tokens, norm1_gain, norm1_bias, weights, so_far
     )
+    projected, their_cotangent = lax.optimization_barrier((projected, their_cotangent))
     mixed, attended, lse, *masks = attend(place, projected, taps, segment_ids)
     masks = (taps, *masks)
 

time: 313 us -> 309 us (0.987)
  Pallas kernels: 190 us -> 186 us
  waiting for transfers between devices: 46.2 us -> 50 us
    convert_element_type x15 -> x9, other arithmetic: 23 us -> 15.5 us  [total(): return result.astype(BF16)]
    add x0 -> x6, other arithmetic: none -> 6.99 us  [total(): return self.terms[0][low:high] + self.terms[1][low:high]]
    pallas_call x4, Pallas kernels: 64.6 us -> 60.3 us  [feed(): pl.pallas_call(functools.partial(feed_kernel, number, int(other), first,...]
    ppermute x34, waiting for transfers between devices: 46.2 us -> 50 us  [send(): return lax.ppermute(values, ('dp', 'mp'), self.pairs)]
  transfers between devices with their start and end apart: 39 -> 39, of which waited for: 11 -> 12; matrix products, arithmetic and copies ran while one was open for 9% -> 8% of each run, Pallas kernels for 55% -> 46%
where the time goes in v1:
time: 309 us; the launch traced here: 308 us
  Pallas kernels  186 us (60%)
  waiting for transfers between devices  50 us (16%)
  other arithmetic  35.9 us (12%)
  starting transfers between devices  32 us (10%)
  local copies, waits for them, and re-layouts  3.09 us (1%)
    pallas_call x4, Pallas kernels, feed(): pl.pallas_call(functools.partial(feed_kernel, number, int(other), first,...  60.3 us
    ppermute x34, waiting for transfers between devices, send(): return lax.ppermute(values, ('dp', 'mp'), self.pairs)  50 us
    pallas_call x2, Pallas kernels, attend_back(): pl.pallas_call(functools.partial(attend_back_kernel, bool(so_far)), grid=...  37.7 us
    ppermute x34, starting transfers between devices, send(): return lax.ppermute(values, ('dp', 'mp'), self.pairs)  28.3 us
    pallas_call x1, Pallas kernels, attend(): pl.pallas_call(attend_kernel, grid_spec=pltpu.PrefetchScalarGridSpec(num_...  25.7 us
    pallas_call x2, Pallas kernels, spread(): pl.pallas_call(spread_kernel, grid_spec=pltpu.PrefetchScalarGridSpec(num_...  18.3 us
    convert_element_type x9, other arithmetic, total(): return result.astype(BF16)  15.5 us
    pallas_call x2, Pallas kernels, front(): pl.pallas_call(functools.partial(front_kernel, bool(so_far)), grid_spec=p...  13.6 us
  transfers between devices with their start and end apart: 39, of which 12 were waited for; matrix products, arithmetic and copies ran while one was open for 8% of the time, Pallas kernels for 46%

profile of v1, /device:TPU:0, one launch (start us, length us, event | category | flops | bytes accessed | tf_op | source)
XLA Modules:
  0.0 307.9 jit_solution(13467685486667156288)
XLA Ops:
  2.6 6.8 %front.2 = (bf16[1024,2304]{1,0:T(8,128)(2,1)}, bf16[1024,768]{1,0:T(8,128)(2,1)}, bf16[1024,768]{1,0:T(8,128)(2,1)}) custom-call(s32[4]{0:T(128)} %pad_add_fusion.place, bf16[2,512,768]{2,1,0:T(8,128)(2,1)} %refs_0_.2, f32[768]{0:T(1024)} %gain.3, f32[768]{0:T(1024)} %refs_5_.5, bf16[3,768,768]{2,1,0:T(8,128)(2,1)} %bitcast.27), custom_call_target="tpu_custom_call" | custom-call | flops 1811939328 | bytes 9043968 | tf_op jit(solution)/shard_map/front/pallas_call | solution.py:303
  9.9 2.6 collective-permute-start.3
  12.5 6.8 %front.3 = (bf16[1024,2304]{1,0:T(8,128)(2,1)}, bf16[1024,768]{1,0:T(8,128)(2,1)}, bf16[1024,768]{1,0:T(8,128)(2,1)}) custom-call(s32[4]{0:T(128)} %pad_add_fusion.place, bf16[1024,2304]{1,0:T(8,128)(2,1)} %get-tuple-element.113.refs_0_, bf16[1024,768]{1,0:T(8,128)(2,1)} %get-tuple-element.114.refs_1_, ...), custom_call_target="tpu_custom_call", output_to_operand_aliasing={{0}: (1, {}), {1}: (2, {}), {2}: (3, {})} | custom-call | flops 1811939328 | bytes 9043968 | tf_op jit(solution)/shard_map/front/pallas_call | solution.py:303
  20.3 25.7 %attend.1 = (bf16[3,1024,768]{2,1,0:T(8,128)(2,1)}, bf16[1024,768]{1,0:T(8,128)(2,1)}, f32[6,2,1024]{2,1,0:T(2,128)}, f32[2,1024,128]{2,1,0:T(8,128)}, s32[1024,128]{1,0:T(8,128)}, /*index=5*/s32[8,1024]{1,0:T(8,128)}) custom-call(s32[4]{0:T(128)} %pad_add_fusion.place, ...), custom_call_target="tpu_custom_call" | custom-call | flops 3221225472 | bytes 12582912 | tf_op jit(solution)/shard_map/attend/pallas_call | solution.py:201
  46.0 17.4 %feed.4 = (f32[1024,768]{1,0:T(8,128)}, bf16[1024,768]{1,0:T(8,128)(2,1)}, bf16[1024,768]{1,0:T(8,128)(2,1)}, bf16[8,2,96,768]{3,2,1,0:T(8,128)(2,1)}, f32[1024,768]{1,0:T(8,128)}, /*index=5*/f32[1024,768]{1,0:T(8,128)}) custom-call(s32[4]{0:T(128)} %pad_add_fusion.place, f32[768]{0:T(1024)} %gain.2, f32[768]{0:T(1024)} %refs_1_.3, ...), custom_call_target="tpu_custom_call" | custom-call | flops 7247757312 | bytes 17301504 | tf_op jit(solution)/shard_map/feed/pallas_call | solution.py:495
  63.7 14.2 %feed.5 = (bf16[8,2,96,768]{3,2,1,0:T(8,128)(2,1)}, f32[1024,768]{1,0:T(8,128)}, f32[1024,768]{1,0:T(8,128)}) custom-call(s32[4]{0:T(128)} %pad_add_fusion.place, bf16[1024,768]{1,0:T(8,128)(2,1)} %get-tuple-element.123.refs_0_, f32[1024,768]{1,0:T(8,128)} %get-tuple-element.127.refs_1_, f32[1024,768]{1,0:T(8,128)} %get-tuple-element.128.refs_2_, ...), custom_call_target="tpu_custom_call" | custom-call | flops 7247757312 | bytes 17301504 | tf_op jit(solution)/shard_map/feed/pallas_call | solution.py:495
  77.9 2.2 slice_add_fusion.2
  80.2 2.0 collective-permute-start.6
  82.1 14.4 %feed.6 = (bf16[8,2,96,768]{3,2,1,0:T(8,128)(2,1)}, f32[1024,768]{1,0:T(8,128)}, f32[1024,768]{1,0:T(8,128)}) custom-call(s32[4]{0:T(128)} %pad_add_fusion.place, bf16[1024,768]{1,0:T(8,128)(2,1)} %get-tuple-element.123.refs_0_, f32[1024,768]{1,0:T(8,128)} %get-tuple-element.135.refs_1_, f32[1024,768]{1,0:T(8,128)} %get-tuple-element.136.refs_2_, ...), custom_call_target="tpu_custom_call" | custom-call | flops 7247757312 | bytes 17301504 | tf_op jit(solution)/shard_map/feed/pallas_call | solution.py:495
  96.6 1.5 add_convert_fusion.2
  98.1 2.0 collective-permute-start.7
  100.1 14.3 %feed.7 = (bf16[8,2,96,768]{3,2,1,0:T(8,128)(2,1)}, bf16[512,768]{1,0:T(8,128)(2,1)}, bf16[512,768]{1,0:T(8,128)(2,1)}, f32[1024,768]{1,0:T(8,128)}) custom-call(s32[4]{0:T(128)} %pad_add_fusion.place, bf16[1024,768]{1,0:T(8,128)(2,1)} %get-tuple-element.123.refs_0_, f32[1024,768]{1,0:T(8,128)} %get-tuple-element.140.refs_1_, ...), custom_call_target="tpu_custom_call" | custom-call | flops 7247757312 | bytes 17301504 | tf_op jit(solution)/shard_map/feed/pallas_call | solution.py:495
  114.4 2.2 add_convert_fusion.8
  116.6 1.4 slice_add_fusion.1
  118.0 1.6 collective-permute-start.10
  119.6 1.6 collective-permute-start.9
  121.2 8.0 %middle.1 = (f32[1024,768]{1,0:T(8,128)}, bf16[1024,768]{1,0:T(8,128)(2,1)}, bf16[1024,768]{1,0:T(8,128)(2,1)}, f32[2,768]{1,0:T(2,128)}) custom-call(f32[1024,768]{1,0:T(8,128)} %get-tuple-element.151.resid, f32[1024,768]{1,0:T(8,128)} %get-tuple-element.152.gradient, bf16[1024,768]{1,0:T(8,128)(2,1)} %get-tuple-element.129.refs_3_.grads, ...), custom_call_target="tpu_custom_call" | custom-call | flops 1207959552 | bytes 14155776 | tf_op jit(solution)/shard_map/middle/pallas_call | solution.py:528
  129.1 2.2 add_convert_fusion.7
  131.3 3.1 collective-permute-done.10
  134.4 2.3 add_convert_fusion.1
  136.8 3.0 collective-permute-start.12
  139.8 18.8 %attend_back.2 = (bf16[3,1024,768]{2,1,0:T(8,128)(2,1)}, f32[9,768]{1,0:T(8,128)}) custom-call(bf16[3,1024,768]{2,1,0:T(8,128)(2,1)} %get-tuple-element.158.refs_0_.refs_2_, bf16[1024,768]{1,0:T(8,128)(2,1)} %get-tuple-element.166.refs_1_.refs_3_, bf16[1024,768]{1,0:T(8,128)(2,1)} %get-tuple-element.121.refs_3_.refs_2_.refs_4_.attended, ...), custom_call_target="tpu_custom_call" | custom-call | flops 4026531840 | bytes 8650752 | tf_op jit(solution)/shard_map/attend_back/pallas_call | solution.py:247
  160.8 1.6 collective-permute-start.15
  162.9 19.0 %attend_back.3 = (bf16[3,1024,768]{2,1,0:T(8,128)(2,1)}, f32[9,768]{1,0:T(8,128)}) custom-call(bf16[3,1024,768]{2,1,0:T(8,128)(2,1)} %get-tuple-element.163.refs_0_, f32[9,768]{1,0:T(8,128)} %get-tuple-element.167.refs_1_, bf16[3,1024,768]{2,1,0:T(8,128)(2,1)} %get-tuple-element.158.refs_0_.refs_2_, ...), custom_call_target="tpu_custom_call", output_to_operand_aliasing={{0}: (0, {}), {1}: (1, {})} | custom-call | flops 4026531840 | bytes 8650752 | tf_op jit(solution)/shard_map/attend_back/pallas_call | solution.py:247
  184.2 1.6 collective-permute-start.16
  186.1 11.5 %weight_grad.1 = (bf16[8,192,768]{2,1,0:T(8,128)(2,1)}, bf16[8,192,768]{2,1,0:T(8,128)(2,1)}) custom-call(s32[4]{0:T(128)} %pad_add_fusion.place, bf16[3,1024,768]{2,1,0:T(8,128)(2,1)} %get-tuple-element.175.back, bf16[1024,768]{1,0:T(8,128)(2,1)} %get-tuple-element.170.normed, bf16[1024,768]{1,0:T(8,128)(2,1)} %get-tuple-element.121.refs_3_.refs_2_.refs_4_.attended, ...), custom_call_target="tpu_custom_call" | custom-call | flops 4831838208 | bytes 15728640 | tf_op jit(solution)/shard_map/weight_grad/pallas_call | solution.py:567
  197.7 2.1 collective-permute-done.17
  201.4 10.7 %last.1 = (bf16[512,768]{1,0:T(8,128)(2,1)}, f32[512,768]{1,0:T(8,128)}, f32[2,768]{1,0:T(2,128)}) custom-call(s32[4]{0:T(128)} %pad_add_fusion.place, bf16[3,1024,768]{2,1,0:T(8,128)(2,1)} %get-tuple-element.175.back, bf16[3,768,768]{2,1,0:T(8,128)(2,1)} %bitcast.29, bf16[1024,768]{1,0:T(8,128)(2,1)} %get-tuple-element.117.refs_2_.tokens, ...), custom_call_target="tpu_custom_call" | custom-call | flops 3623878656 | bytes 16121856 | tf_op jit(solution)/shard_map/last/pallas_call | solution.py:672
  213.0 1.5 slice_add_fusion
  214.4 2.7 collective-permute-done.19.refs_1_
  218.3 3.4 %collective-permute-done.21 = f32[13,768]{1,0:T(8,128)S(1)} collective-permute-done((f32[13,768]{1,0:T(8,128)S(1)}, f32[13,768]{1,0:T(8,128)S(1)}, u32[]{:S(2)}, u32[]{:S(2)}) %collective-permute-start.21) | collective-permute-done | bytes 39968 | tf_op jit(solution)/shard_map/ppermute | solution.py:715
  221.8 11.6 %collective-permute-done.20 = bf16[4,192,768]{2,1,0:T(8,128)(2,1)S(1)} collective-permute-done((bf16[4,192,768]{2,1,0:T(8,128)(2,1)S(1)}, bf16[4,192,768]{2,1,0:T(8,128)(2,1)S(1)}, u32[]{:S(2)}, u32[]{:S(2)}) %collective-permute-start.20) | collective-permute-done | bytes 1179680 | tf_op jit(solution)/shard_map/ppermute | solution.py:715
  233.4 1.7 add_convert_fusion
  235.2 1.4 collective-permute-start.24
  237.3 7.6 %collective-permute-done.25 = bf16[1,2,96,768]{3,2,1,0:T(8,128)(2,1)S(1)} collective-permute-done((bf16[1,2,96,768]{3,2,1,0:T(8,128)(2,1)S(1)}, bf16[1,2,96,768]{3,2,1,0:T(8,128)(2,1)S(1)}, u32[]{:S(2)}, u32[]{:S(2)}) %collective-permute-start.25) | collective-permute-done | bytes 294944 | tf_op jit(solution)/shard_map/ppermute | solution.py:715
  246.6 1.8 add_convert_fusion.4
  249.5 1.4 collective-permute-start.29
  251.7 9.1 %spread.2 = (f32[3072,768]{1,0:T(8,128)}, f32[768,3072]{1,0:T(8,128)}) custom-call(s32[4]{0:T(128)} %pad_add_fusion.place, bf16[4,2,96,768]{3,2,1,0:T(8,128)(2,1)} %copy-done.1, bf16[4,2,96,768]{3,2,1,0:T(8,128)(2,1)} %collective-permute-done.19.refs_1_, bf16[4,2,96,768]{3,2,1,0:T(8,128)(2,1)} %copy-done.7, bf16[4,2,96,768]{3,2,1,0:T(8,128)(2,1)} %copy-done.8), custom_call_target="tpu_custom_call" | custom-call | bytes 14155776 | tf_op jit(solution)/shard_map/spread/pallas_call | solution.py:618
  261.7 1.3 add_convert_fusion.3
  265.5 1.8 collective-permute-start.31
  267.5 4.9 %collective-permute-done.33 = f32[13,768]{1,0:T(8,128)S(1)} collective-permute-done((f32[13,768]{1,0:T(8,128)S(1)}, f32[13,768]{1,0:T(8,128)S(1)}, u32[]{:S(2)}, u32[]{:S(2)}) %collective-permute-start.33) | collective-permute-done | bytes 39968 | tf_op jit(solution)/shard_map/ppermute | solution.py:715
  272.4 7.1 %collective-permute-done.31 = bf16[1,192,768]{2,1,0:T(8,128)(2,1)S(1)} collective-permute-done((bf16[1,192,768]{2,1,0:T(8,128)(2,1)S(1)}, bf16[1,192,768]{2,1,0:T(8,128)(2,1)S(1)}, u32[]{:S(2)}, u32[]{:S(2)}) %collective-permute-start.31) | collective-permute-done | bytes 294944 | tf_op jit(solution)/shard_map/ppermute | solution.py:715
  281.0 2.0 collective-permute-start.35
  283.0 2.8 broadcast_select_fusion.1
  286.4 4.7 %collective-permute-done.35 = bf16[1,192,768]{2,1,0:T(8,128)(2,1)S(1)} collective-permute-done((bf16[1,192,768]{2,1,0:T(8,128)(2,1)S(1)}, bf16[1,192,768]{2,1,0:T(8,128)(2,1)S(1)}, u32[]{:S(2)}, u32[]{:S(2)}) %collective-permute-start.35) | collective-permute-done | bytes 294944 | tf_op jit(solution)/shard_map/ppermute | solution.py:715
  292.4 1.9 broadcast_select_fusion
  295.6 9.2 %spread.3 = (f32[3072,768]{1,0:T(8,128)}, f32[768,3072]{1,0:T(8,128)}) custom-call(s32[4]{0:T(128)} %pad_add_fusion.place, bf16[4,2,96,768]{3,2,1,0:T(8,128)(2,1)} %copy-done, bf16[4,2,96,768]{3,2,1,0:T(8,128)(2,1)} %copy-done.6, bf16[4,2,96,768]{3,2,1,0:T(8,128)(2,1)} %collective-permute-done.36.refs_2_, ...), custom_call_target="tpu_custom_call", output_to_operand_aliasing={{0}: (5, {}), {1}: (6, {})} | custom-call | bytes 14155776 | tf_op jit(solution)/shard_map/spread/pallas_call | solution.py:618
  306.6 1.3 convert_bitcast_fusion
  (119 shorter events, 27.1 us)
Async XLA Ops:
  0.6 8.8 %collective-permute-start = (bf16[2,512,768]{2,1,0:T(8,128)(2,1)}, bf16[2,512,768]{2,1,0:T(8,128)(2,1)S(1)}, u32[]{:S(2)}, u32[]{:S(2)}) collective-permute-start(bf16[2,512,768]{2,1,0:T(8,128)(2,1)} %refs_0_.2), channel_id=1, source_target_pairs={{0,1},{1,0},{2,3},{3,2},{4,5},{5,4},{6,7},{7,6},{8,9},{9,8},{10,11... | collective-permute-start | bytes 4718600 | tf_op jit(solution)/shard_map/ppermute | solution.py:706
  1.2 18.1 %collective-permute-start.1 = (bf16[2,512,768]{2,1,0:T(8,128)(2,1)}, bf16[2,512,768]{2,1,0:T(8,128)(2,1)S(1)}, u32[]{:S(2)}, u32[]{:S(2)}) collective-permute-start(bf16[2,512,768]{2,1,0:T(8,128)(2,1)} %refs_5_.6), channel_id=1, source_target_pairs={{0,1},{1,0},{2,3},{3,2},{4,5},{5,4},{6,7},{7,6},{8,9},{9,8},{10,11... | collective-permute-start | bytes 4718600 | tf_op jit(solution)/shard_map/ppermute | solution.py:706
  9.4 9.9 %collective-permute-start.2 = (f32[9,192]{1,0:T(8,128)S(1)}, f32[9,192]{1,0:T(8,128)S(1)}, u32[]{:S(2)}, u32[]{:S(2)}) collective-permute-start(f32[9,192]{1,0:T(8,128)S(1)} %reshape.39), channel_id=1, source_target_pairs={{0,1},{1,0},{2,3},{3,2},{4,5},{5,4},{6,7},{7,6},{8,9},{9,8},{10,11... | collective-permute-start | bytes 20744 | tf_op jit(solution)/shard_map/ppermute | solution.py:838
  9.9 9.4 %collective-permute-start.3 = (f32[9,192]{1,0:T(8,128)S(1)}, f32[9,192]{1,0:T(8,128)S(1)}, u32[]{:S(2)}, u32[]{:S(2)}) collective-permute-start(f32[9,192]{1,0:T(8,128)S(1)} %reshape.39), channel_id=1, source_target_pairs={{0,2},{1,3},{2,0},{3,1},{4,6},{5,7},{6,4},{7,5},{8,10},{9,11},{10,... | collective-permute-start | bytes 20744 | tf_op jit(solution)/shard_map/ppermute | solution.py:838
  12.5 6.9 %collective-permute-start.4 = (f32[9,192]{1,0:T(8,128)S(1)}, f32[9,192]{1,0:T(8,128)S(1)}, u32[]{:S(2)}, u32[]{:S(2)}) collective-permute-start(f32[9,192]{1,0:T(8,128)S(1)} %reshape.39), channel_id=1, source_target_pairs={{0,3},{1,2},{2,1},{3,0},{4,7},{5,6},{6,5},{7,4},{8,11},{9,10},{10,... | collective-permute-start | bytes 20744 | tf_op jit(solution)/shard_map/ppermute | solution.py:838
  19.3 26.7 %copy-start.15 = (bf16[2,512,768]{2,1,0:T(8,128)(2,1)}, bf16[2,512,768]{2,1,0:T(8,128)(2,1)S(1)}, u32[]{:S(2)}) copy-start(bf16[2,512,768]{2,1,0:T(8,128)(2,1)S(1)} %collective-permute-done.1.refs_6_) | copy-start | bytes 4718596
  63.5 14.4 %collective-permute-start.5 = (bf16[8,2,96,768]{3,2,1,0:T(8,128)(2,1)}, bf16[8,2,96,768]{3,2,1,0:T(8,128)(2,1)S(1)}, u32[]{:S(2)}, u32[]{:S(2)}) collective-permute-start(bf16[8,2,96,768]{3,2,1,0:T(8,128)(2,1)} %get-tuple-element.131), channel_id=1, source_target_pairs={{0,1},{1,0},{2,3},{3,2},{4,5},{5,4},{6,7},{7,6},{8,9},{9,8},{10,11... | collective-permute-start | bytes 7077896 | tf_op jit(solution)/shard_map/ppermute | solution.py:715
  77.9 18.7 %copy-start.3 = (bf16[8,2,96,768]{3,2,1,0:T(8,128)(2,1)}, bf16[8,2,96,768]{3,2,1,0:T(8,128)(2,1)S(1)}, u32[]{:S(2)}) copy-start(bf16[8,2,96,768]{3,2,1,0:T(8,128)(2,1)S(1)} %collective-permute-done.5) | copy-start | bytes 7077892
  80.2 16.4 %collective-permute-start.6 = (bf16[4,2,96,768]{3,2,1,0:T(8,128)(2,1)S(1)}, bf16[4,2,96,768]{3,2,1,0:T(8,128)(2,1)}, u32[]{:S(2)}, u32[]{:S(2)}) collective-permute-start(bf16[4,2,96,768]{3,2,1,0:T(8,128)(2,1)S(1)} %slice_add_fusion.2), channel_id=1, source_target_pairs={{0,4},{1,3},{2,6},{3,1},{4,0},{5,7},{6,2},{7,5},{8,12},{9,11},{10,... | collective-permute-start | bytes 3538952 | tf_op jit(solution)/shard_map/ppermute | solution.py:715
  98.1 18.6 %collective-permute-start.8 = (bf16[8,2,96,768]{3,2,1,0:T(8,128)(2,1)}, bf16[8,2,96,768]{3,2,1,0:T(8,128)(2,1)S(1)}, u32[]{:S(2)}, u32[]{:S(2)}) collective-permute-start(bf16[8,2,96,768]{3,2,1,0:T(8,128)(2,1)} %get-tuple-element.145), channel_id=1, source_target_pairs={{0,1},{1,0},{2,3},{3,2},{4,5},{5,4},{6,7},{7,6},{8,9},{9,8},{10,11... | collective-permute-start | bytes 7077896 | tf_op jit(solution)/shard_map/ppermute | solution.py:715
  98.1 16.2 %collective-permute-start.7 = (bf16[2,2,96,768]{3,2,1,0:T(8,128)(2,1)S(1)}, bf16[2,2,96,768]{3,2,1,0:T(8,128)(2,1)S(1)}, u32[]{:S(2)}, u32[]{:S(2)}) collective-permute-start(bf16[2,2,96,768]{3,2,1,0:T(8,128)(2,1)S(1)} %add_convert_fusion.2), channel_id=1, source_target_pairs={{0,2},{1,5},{2,0},{3,7},{4,6},{5,1},{6,4},{7,3},{8,10},{9,13},{10,... | collective-permute-start | bytes 1769480 | tf_op jit(solution)/shard_map/ppermute | solution.py:715
  118.0 16.4 %collective-permute-start.10 = (bf16[4,2,96,768]{3,2,1,0:T(8,128)(2,1)S(1)}, bf16[4,2,96,768]{3,2,1,0:T(8,128)(2,1)}, u32[]{:S(2)}, u32[]{:S(2)}) collective-permute-start(bf16[4,2,96,768]{3,2,1,0:T(8,128)(2,1)S(1)} %slice_add_fusion.1), channel_id=1, source_target_pairs={{0,4},{1,3},{2,6},{3,1},{4,0},{5,7},{6,2},{7,5},{8,12},{9,11},{10,... | collective-permute-start | bytes 3538952 | tf_op jit(solution)/shard_map/ppermute | solution.py:715
  119.6 9.5 %collective-permute-start.9 = (bf16[1,2,96,768]{3,2,1,0:T(8,128)(2,1)}, bf16[1,2,96,768]{3,2,1,0:T(8,128)(2,1)}, u32[]{:S(2)}, u32[]{:S(2)}) collective-permute-start(bf16[1,2,96,768]{3,2,1,0:T(8,128)(2,1)} %add_convert_fusion.8), channel_id=1, source_target_pairs={{0,8},{1,9},{2,10},{3,11},{4,12},{5,13},{6,14},{7,15},{8,0},{9,1},... | collective-permute-start | bytes 884744 | tf_op jit(solution)/shard_map/ppermute | solution.py:715
  121.1 15.5 %collective-permute-start.11 = (bf16[512,768]{1,0:T(8,128)(2,1)}, bf16[512,768]{1,0:T(8,128)(2,1)}, u32[]{:S(2)}, u32[]{:S(2)}) collective-permute-start(bf16[512,768]{1,0:T(8,128)(2,1)} %get-tuple-element.150), channel_id=1, source_target_pairs={{0,1},{1,0},{2,3},{3,2},{4,5},{5,4},{6,7},{7,6},{8,9},{9,8},{10,11... | collective-permute-start | bytes 2359304 | tf_op jit(solution)/shard_map/ppermute | solution.py:715
  136.7 22.9 %collective-permute-start.13 = (bf16[2,2,96,768]{3,2,1,0:T(8,128)(2,1)}, bf16[2,2,96,768]{3,2,1,0:T(8,128)(2,1)S(1)}, u32[]{:S(2)}, u32[]{:S(2)}) collective-permute-start(bf16[2,2,96,768]{3,2,1,0:T(8,128)(2,1)} %add_convert_fusion.1), channel_id=1, source_target_pairs={{0,2},{1,5},{2,0},{3,7},{4,6},{5,1},{6,4},{7,3},{8,10},{9,13},{10,... | collective-permute-start | bytes 1769480 | tf_op jit(solution)/shard_map/ppermute | solution.py:715
  136.8 21.7 %collective-permute-start.12 = (bf16[1,2,96,768]{3,2,1,0:T(8,128)(2,1)}, bf16[1,2,96,768]{3,2,1,0:T(8,128)(2,1)S(1)}, u32[]{:S(2)}, u32[]{:S(2)}) collective-permute-start(bf16[1,2,96,768]{3,2,1,0:T(8,128)(2,1)} %add_convert_fusion.7), channel_id=1, source_target_pairs={{0,16},{1,17},{2,18},{3,19},{4,20},{5,21},{6,22},{7,23},{8,24},{9,... | collective-permute-start | bytes 884744 | tf_op jit(solution)/shard_map/ppermute | solution.py:715
  160.8 21.1 %collective-permute-start.15 = (bf16[1,2,96,768]{3,2,1,0:T(8,128)(2,1)S(1)}, bf16[1,2,96,768]{3,2,1,0:T(8,128)(2,1)}, u32[]{:S(2)}, u32[]{:S(2)}) collective-permute-start(bf16[1,2,96,768]{3,2,1,0:T(8,128)(2,1)S(1)} %add_convert_fusion.6), channel_id=1, source_target_pairs={{0,8},{1,9},{2,10},{3,11},{4,12},{5,13},{6,14},{7,15},{8,0},{9,1},... | collective-permute-start | bytes 884744 | tf_op jit(solution)/shard_map/ppermute | solution.py:715
  162.4 20.8 %collective-permute-start.14 = (bf16[1,2,96,768]{3,2,1,0:T(8,128)(2,1)S(1)}, bf16[1,2,96,768]{3,2,1,0:T(8,128)(2,1)}, u32[]{:S(2)}, u32[]{:S(2)}) collective-permute-start(bf16[1,2,96,768]{3,2,1,0:T(8,128)(2,1)S(1)} %add.182), channel_id=1, source_target_pairs={{0,8},{1,9},{2,10},{3,11},{4,12},{5,13},{6,14},{7,15},{8,0},{9,1},... | collective-permute-start | bytes 884744 | tf_op jit(solution)/shard_map/ppermute | solution.py:715
  184.2 16.4 %collective-permute-start.16 = (bf16[2,2,96,768]{3,2,1,0:T(8,128)(2,1)S(1)}, bf16[2,2,96,768]{3,2,1,0:T(8,128)(2,1)S(1)}, u32[]{:S(2)}, u32[]{:S(2)}) collective-permute-start(bf16[2,2,96,768]{3,2,1,0:T(8,128)(2,1)S(1)} %pad_maximum_fusion.2), channel_id=1, source_target_pairs={{0,2},{1,5},{2,0},{3,7},{4,6},{5,1},{6,4},{7,3},{8,10},{9,13},{10,... | collective-permute-start | bytes 1769480 | tf_op jit(solution)/shard_map/ppermute | solution.py:715
  185.8 14.0 %collective-permute-start.17 = (bf16[1,2,96,768]{3,2,1,0:T(8,128)(2,1)S(1)}, bf16[1,2,96,768]{3,2,1,0:T(8,128)(2,1)S(1)}, u32[]{:S(2)}, u32[]{:S(2)}) collective-permute-start(bf16[1,2,96,768]{3,2,1,0:T(8,128)(2,1)S(1)} %add_convert_fusion.5), channel_id=1, source_target_pairs={{0,16},{1,17},{2,18},{3,19},{4,20},{5,21},{6,22},{7,23},{8,24},{9,... | collective-permute-start | bytes 884744 | tf_op jit(solution)/shard_map/ppermute | solution.py:715
  200.7 17.0 %copy-start.1 = (bf16[4,2,96,768]{3,2,1,0:T(8,128)(2,1)}, bf16[4,2,96,768]{3,2,1,0:T(8,128)(2,1)S(1)}, u32[]{:S(2)}) copy-start(bf16[4,2,96,768]{3,2,1,0:T(8,128)(2,1)S(1)} %pad_maximum_fusion.refs_0_) | copy-start | bytes 3538948
  200.7 12.2 %collective-permute-start.18 = (bf16[8,192,768]{2,1,0:T(8,128)(2,1)}, bf16[8,192,768]{2,1,0:T(8,128)(2,1)}, u32[]{:S(2)}, u32[]{:S(2)}) collective-permute-start(bf16[8,192,768]{2,1,0:T(8,128)(2,1)} %get-tuple-element.179), channel_id=1, source_target_pairs={{0,1},{1,0},{2,3},{3,2},{4,5},{5,4},{6,7},{7,6},{8,9},{9,8},{10,11... | collective-permute-start | bytes 7077896 | tf_op jit(solution)/shard_map/ppermute | solution.py:715
  200.8 16.4 %collective-permute-start.19 = (bf16[4,2,96,768]{3,2,1,0:T(8,128)(2,1)S(1)}, bf16[4,2,96,768]{3,2,1,0:T(8,128)(2,1)}, u32[]{:S(2)}, u32[]{:S(2)}) collective-permute-start(bf16[4,2,96,768]{3,2,1,0:T(8,128)(2,1)S(1)} %pad_maximum_fusion.refs_0_), channel_id=1, source_target_pairs={{0,4},{1,3},{2,6},{3,1},{4,0},{5,7},{6,2},{7,5},{8,12},{9,11},{10,... | collective-permute-start | bytes 3538952 | tf_op jit(solution)/shard_map/ppermute | solution.py:715
  201.4 11.6 %copy-start.2 = (bf16[8,192,768]{2,1,0:T(8,128)(2,1)S(1)}, bf16[8,192,768]{2,1,0:T(8,128)(2,1)}, u32[]{:S(2)}) copy-start(bf16[8,192,768]{2,1,0:T(8,128)(2,1)} %get-tuple-element.178) | copy-start | bytes 7077892
  214.4 22.2 %copy-start.9 = (bf16[1,2,96,768]{3,2,1,0:T(8,128)(2,1)S(1)}, bf16[1,2,96,768]{3,2,1,0:T(8,128)(2,1)}, u32[]{:S(2)}) copy-start(bf16[1,2,96,768]{3,2,1,0:T(8,128)(2,1)} %add.190) | copy-start | bytes 884740
  217.2 16.2 %collective-permute-start.20 = (bf16[4,192,768]{2,1,0:T(8,128)(2,1)S(1)}, bf16[4,192,768]{2,1,0:T(8,128)(2,1)S(1)}, u32[]{:S(2)}, u32[]{:S(2)}) collective-permute-start(bf16[4,192,768]{2,1,0:T(8,128)(2,1)S(1)} %slice_add_fusion), channel_id=1, source_target_pairs={{0,4},{1,3},{2,6},{3,1},{4,0},{5,7},{6,2},{7,5},{8,12},{9,11},{10,... | collective-permute-start | bytes 3538952 | tf_op jit(solution)/shard_map/ppermute | solution.py:715
  217.7 17.4 %collective-permute-start.22 = (bf16[4,2,96,768]{3,2,1,0:T(8,128)(2,1)S(1)}, bf16[4,2,96,768]{3,2,1,0:T(8,128)(2,1)S(1)}, u32[]{:S(2)}, u32[]{:S(2)}) collective-permute-start(bf16[4,2,96,768]{3,2,1,0:T(8,128)(2,1)S(1)} %pad_maximum_fusion.refs_0_), channel_id=1, source_target_pairs={{0,1},{1,0},{2,3},{3,2},{4,5},{5,4},{6,7},{7,6},{8,9},{9,8},{10,11... | collective-permute-start | bytes 3538952 | tf_op jit(solution)/shard_map/ppermute | solution.py:715
  217.8 17.2 %collective-permute-start.23 = (bf16[512,768]{1,0:T(8,128)(2,1)S(1)}, bf16[512,768]{1,0:T(8,128)(2,1)S(1)}, u32[]{:S(2)}, u32[]{:S(2)}) collective-permute-start(bf16[512,768]{1,0:T(8,128)(2,1)S(1)} %copy-done.16), channel_id=1, source_target_pairs={{0,1},{1,0},{2,3},{3,2},{4,5},{5,4},{6,7},{7,6},{8,9},{9,8},{10,11... | collective-permute-start | bytes 2359304 | tf_op jit(solution)/shard_map/ppermute | solution.py:715
  218.2 3.5 %collective-permute-start.21 = (f32[13,768]{1,0:T(8,128)S(1)}, f32[13,768]{1,0:T(8,128)S(1)}, u32[]{:S(2)}, u32[]{:S(2)}) collective-permute-start(f32[13,768]{1,0:T(8,128)S(1)} %pad_maximum_fusion.7), channel_id=1, source_target_pairs={{0,1},{1,0},{2,3},{3,2},{4,5},{5,4},{6,7},{7,6},{8,9},{9,8},{10,11... | collective-permute-start | bytes 119816 | tf_op jit(solution)/shard_map/ppermute | solution.py:715
  233.4 13.3 %copy-start.10 = (bf16[4,192,768]{2,1,0:T(8,128)(2,1)}, bf16[4,192,768]{2,1,0:T(8,128)(2,1)S(1)}, u32[]{:S(2)}) copy-start(bf16[4,192,768]{2,1,0:T(8,128)(2,1)S(1)} %collective-permute-done.20) | copy-start | bytes 3538948
  235.1 15.8 %copy-start.11 = (bf16[512,768]{1,0:T(8,128)(2,1)}, bf16[512,768]{1,0:T(8,128)(2,1)S(1)}, u32[]{:S(2)}) copy-start(bf16[512,768]{1,0:T(8,128)(2,1)S(1)} %collective-permute-done.23) | copy-start | bytes 2359300
  235.1 13.4 %copy-start.7 = (bf16[4,2,96,768]{3,2,1,0:T(8,128)(2,1)}, bf16[4,2,96,768]{3,2,1,0:T(8,128)(2,1)S(1)}, u32[]{:S(2)}) copy-start(bf16[4,2,96,768]{3,2,1,0:T(8,128)(2,1)S(1)} %collective-permute-done.22.refs_2_) | copy-start | bytes 3538948
  235.1 13.4 %collective-permute-start.27 = (bf16[4,2,96,768]{3,2,1,0:T(8,128)(2,1)}, bf16[4,2,96,768]{3,2,1,0:T(8,128)(2,1)S(1)}, u32[]{:S(2)}, u32[]{:S(2)}) collective-permute-start(bf16[4,2,96,768]{3,2,1,0:T(8,128)(2,1)} %collective-permute-done.19.refs_1_), channel_id=1, source_target_pairs={{0,1},{1,0},{2,3},{3,2},{4,5},{5,4},{6,7},{7,6},{8,9},{9,8},{10,11... | collective-permute-start | bytes 3538952 | tf_op jit(solution)/shard_map/ppermute | solution.py:715
  235.2 11.5 %collective-permute-start.24 = (bf16[2,192,768]{2,1,0:T(8,128)(2,1)S(1)}, bf16[2,192,768]{2,1,0:T(8,128)(2,1)S(1)}, u32[]{:S(2)}, u32[]{:S(2)}) collective-permute-start(bf16[2,192,768]{2,1,0:T(8,128)(2,1)S(1)} %add_convert_fusion), channel_id=1, source_target_pairs={{0,2},{1,5},{2,0},{3,7},{4,6},{5,1},{6,4},{7,3},{8,10},{9,13},{10,... | collective-permute-start | bytes 1769480 | tf_op jit(solution)/shard_map/ppermute | solution.py:715
  236.6 8.3 %collective-permute-start.25 = (bf16[1,2,96,768]{3,2,1,0:T(8,128)(2,1)S(1)}, bf16[1,2,96,768]{3,2,1,0:T(8,128)(2,1)S(1)}, u32[]{:S(2)}, u32[]{:S(2)}) collective-permute-start(bf16[1,2,96,768]{3,2,1,0:T(8,128)(2,1)S(1)} %copy-done.9), channel_id=1, source_target_pairs={{0,8},{1,9},{2,10},{3,11},{4,12},{5,13},{6,14},{7,15},{8,0},{9,1},... | collective-permute-start | bytes 884744 | tf_op jit(solution)/shard_map/ppermute | solution.py:715
  236.6 9.4 %collective-permute-start.26 = (f32[13,768]{1,0:T(8,128)S(1)}, f32[13,768]{1,0:T(8,128)S(1)}, u32[]{:S(2)}, u32[]{:S(2)}) collective-permute-start(f32[13,768]{1,0:T(8,128)S(1)} %add.194), channel_id=1, source_target_pairs={{0,2},{1,3},{2,0},{3,1},{4,6},{5,7},{6,4},{7,5},{8,10},{9,11},{10,... | collective-permute-start | bytes 119816 | tf_op jit(solution)/shard_map/ppermute | solution.py:715
  249.5 13.5 %collective-permute-start.29 = (bf16[2,2,96,768]{3,2,1,0:T(8,128)(2,1)S(1)}, bf16[2,2,96,768]{3,2,1,0:T(8,128)(2,1)}, u32[]{:S(2)}, u32[]{:S(2)}) collective-permute-start(bf16[2,2,96,768]{3,2,1,0:T(8,128)(2,1)S(1)} %pad_maximum_fusion.3), channel_id=1, source_target_pairs={{0,2},{1,5},{2,0},{3,7},{4,6},{5,1},{6,4},{7,3},{8,10},{9,13},{10,... | collective-permute-start | bytes 1769480 | tf_op jit(solution)/shard_map/ppermute | solution.py:715
  250.9 10.8 %collective-permute-start.28 = (bf16[1,192,768]{2,1,0:T(8,128)(2,1)}, bf16[1,192,768]{2,1,0:T(8,128)(2,1)}, u32[]{:S(2)}, u32[]{:S(2)}) collective-permute-start(bf16[1,192,768]{2,1,0:T(8,128)(2,1)} %add_convert_fusion.4), channel_id=1, source_target_pairs={{0,8},{1,9},{2,10},{3,11},{4,12},{5,13},{6,14},{7,15},{8,0},{9,1},... | collective-permute-start | bytes 884744 | tf_op jit(solution)/shard_map/ppermute | solution.py:715
  250.9 9.9 %collective-permute-start.30 = (f32[13,768]{1,0:T(8,128)}, f32[13,768]{1,0:T(8,128)}, u32[]{:S(2)}, u32[]{:S(2)}) collective-permute-start(f32[13,768]{1,0:T(8,128)} %add.201), channel_id=1, source_target_pairs={{0,4},{1,5},{2,6},{3,7},{4,0},{5,1},{6,2},{7,3},{8,12},{9,13},{10,... | collective-permute-start | bytes 119816 | tf_op jit(solution)/shard_map/ppermute | solution.py:715
  264.2 21.6 %copy-start = (bf16[4,2,96,768]{3,2,1,0:T(8,128)(2,1)}, bf16[4,2,96,768]{3,2,1,0:T(8,128)(2,1)S(1)}, u32[]{:S(2)}) copy-start(bf16[4,2,96,768]{3,2,1,0:T(8,128)(2,1)S(1)} %pad_maximum_fusion.1.refs_0_) | copy-start | bytes 3538948
  264.2 16.3 %collective-permute-start.32 = (bf16[4,2,96,768]{3,2,1,0:T(8,128)(2,1)S(1)}, bf16[4,2,96,768]{3,2,1,0:T(8,128)(2,1)S(1)}, u32[]{:S(2)}, u32[]{:S(2)}) collective-permute-start(bf16[4,2,96,768]{3,2,1,0:T(8,128)(2,1)S(1)} %pad_maximum_fusion.1.refs_0_), channel_id=1, source_target_pairs={{0,4},{1,3},{2,6},{3,1},{4,0},{5,7},{6,2},{7,5},{8,12},{9,11},{10,... | collective-permute-start | bytes 3538952 | tf_op jit(solution)/shard_map/ppermute | solution.py:715
  265.5 14.1 %collective-permute-start.31 = (bf16[1,192,768]{2,1,0:T(8,128)(2,1)S(1)}, bf16[1,192,768]{2,1,0:T(8,128)(2,1)S(1)}, u32[]{:S(2)}, u32[]{:S(2)}) collective-permute-start(bf16[1,192,768]{2,1,0:T(8,128)(2,1)S(1)} %add_convert_fusion.3), channel_id=1, source_target_pairs={{0,16},{1,17},{2,18},{3,19},{4,20},{5,21},{6,22},{7,23},{8,24},{9,... | collective-permute-start | bytes 884744 | tf_op jit(solution)/shard_map/ppermute | solution.py:715
  267.3 5.1 %collective-permute-start.33 = (f32[13,768]{1,0:T(8,128)S(1)}, f32[13,768]{1,0:T(8,128)S(1)}, u32[]{:S(2)}, u32[]{:S(2)}) collective-permute-start(f32[13,768]{1,0:T(8,128)S(1)} %add.203), channel_id=1, source_target_pairs={{0,8},{1,9},{2,10},{3,11},{4,12},{5,13},{6,14},{7,15},{8,0},{9,1},... | collective-permute-start | bytes 119816 | tf_op jit(solution)/shard_map/ppermute | solution.py:715
  280.5 10.7 %collective-permute-start.36 = (bf16[4,2,96,768]{3,2,1,0:T(8,128)(2,1)S(1)}, bf16[4,2,96,768]{3,2,1,0:T(8,128)(2,1)}, u32[]{:S(2)}, u32[]{:S(2)}) collective-permute-start(bf16[4,2,96,768]{3,2,1,0:T(8,128)(2,1)S(1)} %pad_maximum_fusion.1.refs_0_), channel_id=1, source_target_pairs={{0,1},{1,0},{2,3},{3,2},{4,5},{5,4},{6,7},{7,6},{8,9},{9,8},{10,11... | collective-permute-start | bytes 3538952 | tf_op jit(solution)/shard_map/ppermute | solution.py:715
  280.5 10.7 %collective-permute-start.37 = (bf16[4,2,96,768]{3,2,1,0:T(8,128)(2,1)S(1)}, bf16[4,2,96,768]{3,2,1,0:T(8,128)(2,1)}, u32[]{:S(2)}, u32[]{:S(2)}) collective-permute-start(bf16[4,2,96,768]{3,2,1,0:T(8,128)(2,1)S(1)} %collective-permute-done.32.refs_1_), channel_id=1, source_target_pairs={{0,1},{1,0},{2,3},{3,2},{4,5},{5,4},{6,7},{7,6},{8,9},{9,8},{10,11... | collective-permute-start | bytes 3538952 | tf_op jit(solution)/shard_map/ppermute | solution.py:715
  281.0 10.1 %collective-permute-start.35 = (bf16[1,192,768]{2,1,0:T(8,128)(2,1)S(1)}, bf16[1,192,768]{2,1,0:T(8,128)(2,1)S(1)}, u32[]{:S(2)}, u32[]{:S(2)}) collective-permute-start(bf16[1,192,768]{2,1,0:T(8,128)(2,1)S(1)} %add.204), channel_id=1, source_target_pairs={{0,8},{1,9},{2,10},{3,11},{4,12},{5,13},{6,14},{7,15},{8,0},{9,1},... | collective-permute-start | bytes 884744 | tf_op jit(solution)/shard_map/ppermute | solution.py:715
  285.9 8.4 %collective-permute-start.34 = (f32[13,768]{1,0:T(8,128)S(1)}, f32[13,768]{1,0:T(8,128)S(1)}, u32[]{:S(2)}, u32[]{:S(2)}) collective-permute-start(f32[13,768]{1,0:T(8,128)S(1)} %add.205), channel_id=1, source_target_pairs={{0,16},{1,17},{2,18},{3,19},{4,20},{5,21},{6,22},{7,23},{8,24},{9,... | collective-permute-start | bytes 119816 | tf_op jit(solution)/shard_map/ppermute | solution.py:715
  291.1 14.5 %collective-permute-start.38 = (bf16[2,192,768]{2,1,0:T(8,128)(2,1)S(1)}, bf16[2,192,768]{2,1,0:T(8,128)(2,1)S(1)}, u32[]{:S(2)}, u32[]{:S(2)}) collective-permute-start(bf16[2,192,768]{2,1,0:T(8,128)(2,1)S(1)} %pad_maximum_fusion.4), channel_id=1, source_target_pairs={{0,4},{1,5},{2,6},{3,7},{4,0},{5,1},{6,2},{7,3},{8,12},{9,13},{10,... | collective-permute-start | bytes 1769480 | tf_op jit(solution)/shard_map/ppermute | solution.py:715
  (8 other events, 36.7 us)

commit v2 on v1

--- a/solution.py
+++ b/solution.py
@@ -943,8 +943,8 @@
         (("core", "a", "b"), (), chunk_last),
         (("h", "a0", "in", "small"), ("a",), None),
         (("h", "a1", "small"), ("a0", "in"), None),
-        (("h", "b", "small"), ("a1",), chunk_spread(0, "a")),
-        (("h", "b", "small"), (), None),
+        (("h", "b", "small"), ("a1",), None),
+        (("h", "b", "small"), (), chunk_spread(0, "a")),
         (("h", "b0", "b1", "small"), ("b",), None),
         (("h",), ("b0", "b1"), chunk_spread(1, "b")),
     ]

time: 309 us -> 303 us (0.981)
  waiting for transfers between devices: 50 us -> 46.7 us
    ppermute x34, waiting for transfers between devices: 50 us -> 46.7 us  [send(): return lax.ppermute(values, ('dp', 'mp'), self.pairs)]
  transfers between devices with their start and end apart: 39 -> 39, of which waited for: 12 -> 12; matrix products, arithmetic and copies ran while one was open for 8% -> 8% of each run, Pallas kernels for 46% -> 47%
where the time goes in v2:
time: 303 us; the launch traced here: 302 us
  Pallas kernels  186 us (61%)
  waiting for transfers between devices  46.7 us (15%)
  other arithmetic  33.5 us (11%)
  starting transfers between devices  32.7 us (11%)
    pallas_call x4, Pallas kernels, feed(): pl.pallas_call(functools.partial(feed_kernel, number, int(other), first,...  60.4 us
    ppermute x34, waiting for transfers between devices, send(): return lax.ppermute(values, ('dp', 'mp'), self.pairs)  46.7 us
    pallas_call x2, Pallas kernels, attend_back(): pl.pallas_call(functools.partial(attend_back_kernel, bool(so_far)), grid=...  37.7 us
    ppermute x34, starting transfers between devices, send(): return lax.ppermute(values, ('dp', 'mp'), self.pairs)  28.9 us
    pallas_call x1, Pallas kernels, attend(): pl.pallas_call(attend_kernel, grid_spec=pltpu.PrefetchScalarGridSpec(num_...  25.8 us
    pallas_call x2, Pallas kernels, spread(): pl.pallas_call(spread_kernel, grid_spec=pltpu.PrefetchScalarGridSpec(num_...  18.3 us
    convert_element_type x9, other arithmetic, total(): return result.astype(BF16)  14.3 us
    pallas_call x2, Pallas kernels, front(): pl.pallas_call(functools.partial(front_kernel, bool(so_far)), grid_spec=p...  13.6 us
  transfers between devices with their start and end apart: 39, of which 12 were waited for; matrix products, arithmetic and copies ran while one was open for 8% of the time, Pallas kernels for 47%

profile of v2, /device:TPU:0, one launch (start us, length us, event | category | flops | bytes accessed | tf_op | source)
XLA Modules:
  0.0 302.1 jit_solution(18412614112434625345)
XLA Ops:
  2.6 6.8 %front.2 = (bf16[1024,2304]{1,0:T(8,128)(2,1)}, bf16[1024,768]{1,0:T(8,128)(2,1)}, bf16[1024,768]{1,0:T(8,128)(2,1)}) custom-call(s32[4]{0:T(128)} %pad_add_fusion.place, bf16[2,512,768]{2,1,0:T(8,128)(2,1)} %refs_0_.2, f32[768]{0:T(1024)} %gain.3, f32[768]{0:T(1024)} %refs_5_.5, bf16[3,768,768]{2,1,0:T(8,128)(2,1)} %bitcast.27), custom_call_target="tpu_custom_call" | custom-call | flops 1811939328 | bytes 9043968 | tf_op jit(solution)/shard_map/front/pallas_call | solution.py:303
  9.9 2.6 collective-permute-start.3
  12.6 6.8 %front.3 = (bf16[1024,2304]{1,0:T(8,128)(2,1)}, bf16[1024,768]{1,0:T(8,128)(2,1)}, bf16[1024,768]{1,0:T(8,128)(2,1)}) custom-call(s32[4]{0:T(128)} %pad_add_fusion.place, bf16[1024,2304]{1,0:T(8,128)(2,1)} %get-tuple-element.113.refs_0_, bf16[1024,768]{1,0:T(8,128)(2,1)} %get-tuple-element.114.refs_1_, ...), custom_call_target="tpu_custom_call", output_to_operand_aliasing={{0}: (1, {}), {1}: (2, {}), {2}: (3, {})} | custom-call | flops 1811939328 | bytes 9043968 | tf_op jit(solution)/shard_map/front/pallas_call | solution.py:303
  20.3 25.8 %attend.1 = (bf16[3,1024,768]{2,1,0:T(8,128)(2,1)}, bf16[1024,768]{1,0:T(8,128)(2,1)}, f32[6,2,1024]{2,1,0:T(2,128)}, f32[2,1024,128]{2,1,0:T(8,128)}, s32[1024,128]{1,0:T(8,128)}, /*index=5*/s32[8,1024]{1,0:T(8,128)}) custom-call(s32[4]{0:T(128)} %pad_add_fusion.place, ...), custom_call_target="tpu_custom_call" | custom-call | flops 3221225472 | bytes 12582912 | tf_op jit(solution)/shard_map/attend/pallas_call | solution.py:201
  46.2 17.4 %feed.4 = (f32[1024,768]{1,0:T(8,128)}, bf16[1024,768]{1,0:T(8,128)(2,1)}, bf16[1024,768]{1,0:T(8,128)(2,1)}, bf16[8,2,96,768]{3,2,1,0:T(8,128)(2,1)}, f32[1024,768]{1,0:T(8,128)}, /*index=5*/f32[1024,768]{1,0:T(8,128)}) custom-call(s32[4]{0:T(128)} %pad_add_fusion.place, f32[768]{0:T(1024)} %gain.2, f32[768]{0:T(1024)} %refs_1_.3, ...), custom_call_target="tpu_custom_call" | custom-call | flops 7247757312 | bytes 17301504 | tf_op jit(solution)/shard_map/feed/pallas_call | solution.py:495
  63.8 14.2 %feed.5 = (bf16[8,2,96,768]{3,2,1,0:T(8,128)(2,1)}, f32[1024,768]{1,0:T(8,128)}, f32[1024,768]{1,0:T(8,128)}) custom-call(s32[4]{0:T(128)} %pad_add_fusion.place, bf16[1024,768]{1,0:T(8,128)(2,1)} %get-tuple-element.123.refs_0_, f32[1024,768]{1,0:T(8,128)} %get-tuple-element.127.refs_1_, f32[1024,768]{1,0:T(8,128)} %get-tuple-element.128.refs_2_, ...), custom_call_target="tpu_custom_call" | custom-call | flops 7247757312 | bytes 17301504 | tf_op jit(solution)/shard_map/feed/pallas_call | solution.py:495
  78.1 2.2 slice_add_fusion.2
  80.3 2.0 collective-permute-start.6
  82.3 14.4 %feed.6 = (bf16[8,2,96,768]{3,2,1,0:T(8,128)(2,1)}, f32[1024,768]{1,0:T(8,128)}, f32[1024,768]{1,0:T(8,128)}) custom-call(s32[4]{0:T(128)} %pad_add_fusion.place, bf16[1024,768]{1,0:T(8,128)(2,1)} %get-tuple-element.123.refs_0_, f32[1024,768]{1,0:T(8,128)} %get-tuple-element.135.refs_1_, f32[1024,768]{1,0:T(8,128)} %get-tuple-element.136.refs_2_, ...), custom_call_target="tpu_custom_call" | custom-call | flops 7247757312 | bytes 17301504 | tf_op jit(solution)/shard_map/feed/pallas_call | solution.py:495
  96.8 1.5 add_convert_fusion.2
  98.3 1.9 collective-permute-start.7
  100.3 14.3 %feed.7 = (bf16[8,2,96,768]{3,2,1,0:T(8,128)(2,1)}, bf16[512,768]{1,0:T(8,128)(2,1)}, bf16[512,768]{1,0:T(8,128)(2,1)}, f32[1024,768]{1,0:T(8,128)}) custom-call(s32[4]{0:T(128)} %pad_add_fusion.place, bf16[1024,768]{1,0:T(8,128)(2,1)} %get-tuple-element.123.refs_0_, f32[1024,768]{1,0:T(8,128)} %get-tuple-element.140.refs_1_, ...), custom_call_target="tpu_custom_call" | custom-call | flops 7247757312 | bytes 17301504 | tf_op jit(solution)/shard_map/feed/pallas_call | solution.py:495
  114.5 2.2 add_convert_fusion.8
  116.8 1.4 slice_add_fusion.1
  118.2 1.5 collective-permute-start.10
  119.7 1.6 collective-permute-start.9
  121.3 7.9 %middle.1 = (f32[1024,768]{1,0:T(8,128)}, bf16[1024,768]{1,0:T(8,128)(2,1)}, bf16[1024,768]{1,0:T(8,128)(2,1)}, f32[2,768]{1,0:T(2,128)}) custom-call(f32[1024,768]{1,0:T(8,128)} %get-tuple-element.151.resid, f32[1024,768]{1,0:T(8,128)} %get-tuple-element.152.gradient, bf16[1024,768]{1,0:T(8,128)(2,1)} %get-tuple-element.129.refs_3_.grads, ...), custom_call_target="tpu_custom_call" | custom-call | flops 1207959552 | bytes 14155776 | tf_op jit(solution)/shard_map/middle/pallas_call | solution.py:528
  129.2 2.2 add_convert_fusion.7
  131.5 3.1 %collective-permute-done.10 = bf16[4,2,96,768]{3,2,1,0:T(8,128)(2,1)} collective-permute-done((bf16[4,2,96,768]{3,2,1,0:T(8,128)(2,1)S(1)}, bf16[4,2,96,768]{3,2,1,0:T(8,128)(2,1)}, u32[]{:S(2)}, u32[]{:S(2)}) %collective-permute-start.10) | collective-permute-done | bytes 1179680 | tf_op jit(solution)/shard_map/ppermute | solution.py:715
  134.5 2.3 add_convert_fusion.1
  137.0 2.9 collective-permute-start.12
  139.9 18.8 %attend_back.2 = (bf16[3,1024,768]{2,1,0:T(8,128)(2,1)}, f32[9,768]{1,0:T(8,128)}) custom-call(bf16[3,1024,768]{2,1,0:T(8,128)(2,1)} %get-tuple-element.158.refs_0_.refs_2_, bf16[1024,768]{1,0:T(8,128)(2,1)} %get-tuple-element.166.refs_1_.refs_3_, bf16[1024,768]{1,0:T(8,128)(2,1)} %get-tuple-element.121.refs_3_.refs_2_.refs_4_.attended, ...), custom_call_target="tpu_custom_call" | custom-call | flops 4026531840 | bytes 8650752 | tf_op jit(solution)/shard_map/attend_back/pallas_call | solution.py:247
  160.9 1.6 collective-permute-start.15
  163.0 19.0 %attend_back.3 = (bf16[3,1024,768]{2,1,0:T(8,128)(2,1)}, f32[9,768]{1,0:T(8,128)}) custom-call(bf16[3,1024,768]{2,1,0:T(8,128)(2,1)} %get-tuple-element.163.refs_0_, f32[9,768]{1,0:T(8,128)} %get-tuple-element.167.refs_1_, bf16[3,1024,768]{2,1,0:T(8,128)(2,1)} %get-tuple-element.158.refs_0_.refs_2_, ...), custom_call_target="tpu_custom_call", output_to_operand_aliasing={{0}: (0, {}), {1}: (1, {})} | custom-call | flops 4026531840 | bytes 8650752 | tf_op jit(solution)/shard_map/attend_back/pallas_call | solution.py:247
  182.0 1.3 add_convert_fusion.5
  184.3 1.6 collective-permute-start.16
  186.3 11.5 %weight_grad.1 = (bf16[8,192,768]{2,1,0:T(8,128)(2,1)}, bf16[8,192,768]{2,1,0:T(8,128)(2,1)}) custom-call(s32[4]{0:T(128)} %pad_add_fusion.place, bf16[3,1024,768]{2,1,0:T(8,128)(2,1)} %get-tuple-element.175.back, bf16[1024,768]{1,0:T(8,128)(2,1)} %get-tuple-element.170.normed, bf16[1024,768]{1,0:T(8,128)(2,1)} %get-tuple-element.121.refs_3_.refs_2_.refs_4_.attended, ...), custom_call_target="tpu_custom_call" | custom-call | flops 4831838208 | bytes 15728640 | tf_op jit(solution)/shard_map/weight_grad/pallas_call | solution.py:567
  197.8 2.1 collective-permute-done.17
  201.5 10.7 %last.1 = (bf16[512,768]{1,0:T(8,128)(2,1)}, f32[512,768]{1,0:T(8,128)}, f32[2,768]{1,0:T(2,128)}) custom-call(s32[4]{0:T(128)} %pad_add_fusion.place, bf16[3,1024,768]{2,1,0:T(8,128)(2,1)} %get-tuple-element.175.back, bf16[3,768,768]{2,1,0:T(8,128)(2,1)} %bitcast.29, bf16[1024,768]{1,0:T(8,128)(2,1)} %get-tuple-element.117.refs_2_.tokens, ...), custom_call_target="tpu_custom_call" | custom-call | flops 3623878656 | bytes 16121856 | tf_op jit(solution)/shard_map/last/pallas_call | solution.py:672
  213.1 1.5 slice_add_fusion
  214.6 2.7 collective-permute-done.19.refs_1_
  218.4 3.4 %collective-permute-done.21 = f32[13,768]{1,0:T(8,128)S(1)} collective-permute-done((f32[13,768]{1,0:T(8,128)S(1)}, f32[13,768]{1,0:T(8,128)S(1)}, u32[]{:S(2)}, u32[]{:S(2)}) %collective-permute-start.21) | collective-permute-done | bytes 39968 | tf_op jit(solution)/shard_map/ppermute | solution.py:715
  221.9 11.6 %collective-permute-done.20 = bf16[4,192,768]{2,1,0:T(8,128)(2,1)S(1)} collective-permute-done((bf16[4,192,768]{2,1,0:T(8,128)(2,1)S(1)}, bf16[4,192,768]{2,1,0:T(8,128)(2,1)S(1)}, u32[]{:S(2)}, u32[]{:S(2)}) %collective-permute-start.20) | collective-permute-done | bytes 1179680 | tf_op jit(solution)/shard_map/ppermute | solution.py:715
  234.9 1.4 collective-permute-start.24
  237.0 7.6 %collective-permute-done.25 = bf16[1,2,96,768]{3,2,1,0:T(8,128)(2,1)S(1)} collective-permute-done((bf16[1,2,96,768]{3,2,1,0:T(8,128)(2,1)S(1)}, bf16[1,2,96,768]{3,2,1,0:T(8,128)(2,1)S(1)}, u32[]{:S(2)}, u32[]{:S(2)}) %collective-permute-start.25) | collective-permute-done | bytes 294944 | tf_op jit(solution)/shard_map/ppermute | solution.py:715
  246.9 1.4 collective-permute-start.29
  249.2 3.8 %collective-permute-done.30 = f32[13,768]{1,0:T(8,128)S(1)} collective-permute-done((f32[13,768]{1,0:T(8,128)S(1)}, f32[13,768]{1,0:T(8,128)S(1)}, u32[]{:S(2)}, u32[]{:S(2)}) %collective-permute-start.30) | collective-permute-done | bytes 39968 | tf_op jit(solution)/shard_map/ppermute | solution.py:715
  253.0 2.3 collective-permute-done.28
  257.7 1.7 collective-permute-start.31
  260.6 9.1 %spread.2 = (f32[3072,768]{1,0:T(8,128)}, f32[768,3072]{1,0:T(8,128)}) custom-call(s32[4]{0:T(128)} %pad_add_fusion.place, bf16[4,2,96,768]{3,2,1,0:T(8,128)(2,1)} %copy-done.1, bf16[4,2,96,768]{3,2,1,0:T(8,128)(2,1)} %collective-permute-done.19.refs_1_, bf16[4,2,96,768]{3,2,1,0:T(8,128)(2,1)} %copy-done.7, bf16[4,2,96,768]{3,2,1,0:T(8,128)(2,1)} %copy-done.8), custom_call_target="tpu_custom_call" | custom-call | bytes 14155776 | tf_op jit(solution)/shard_map/spread/pallas_call | solution.py:618
  270.4 3.7 %collective-permute-done.31 = bf16[1,192,768]{2,1,0:T(8,128)(2,1)S(1)} collective-permute-done((bf16[1,192,768]{2,1,0:T(8,128)(2,1)S(1)}, bf16[1,192,768]{2,1,0:T(8,128)(2,1)S(1)}, u32[]{:S(2)}, u32[]{:S(2)}) %collective-permute-start.31) | collective-permute-done | bytes 294944 | tf_op jit(solution)/shard_map/ppermute | solution.py:715
  274.8 2.8 broadcast_select_fusion.1
  277.7 2.3 collective-permute-start.34
  279.9 4.8 %collective-permute-done.35 = bf16[1,192,768]{2,1,0:T(8,128)(2,1)S(1)} collective-permute-done((bf16[1,192,768]{2,1,0:T(8,128)(2,1)S(1)}, bf16[1,192,768]{2,1,0:T(8,128)(2,1)S(1)}, u32[]{:S(2)}, u32[]{:S(2)}) %collective-permute-start.35) | collective-permute-done | bytes 294944 | tf_op jit(solution)/shard_map/ppermute | solution.py:715
  284.9 1.7 collective-permute-start.38
  286.6 1.9 broadcast_select_fusion
  290.6 9.2 %spread.3 = (f32[3072,768]{1,0:T(8,128)}, f32[768,3072]{1,0:T(8,128)}) custom-call(s32[4]{0:T(128)} %pad_add_fusion.place, bf16[4,2,96,768]{3,2,1,0:T(8,128)(2,1)} %copy-done, bf16[4,2,96,768]{3,2,1,0:T(8,128)(2,1)} %copy-done.6, bf16[4,2,96,768]{3,2,1,0:T(8,128)(2,1)} %collective-permute-done.36.refs_2_, ...), custom_call_target="tpu_custom_call", output_to_operand_aliasing={{0}: (5, {}), {1}: (6, {})} | custom-call | bytes 14155776 | tf_op jit(solution)/shard_map/spread/pallas_call | solution.py:618
  300.7 1.3 convert_bitcast_fusion
  (117 shorter events, 25.0 us)
Async XLA Ops:
  0.6 8.8 %collective-permute-start = (bf16[2,512,768]{2,1,0:T(8,128)(2,1)}, bf16[2,512,768]{2,1,0:T(8,128)(2,1)S(1)}, u32[]{:S(2)}, u32[]{:S(2)}) collective-permute-start(bf16[2,512,768]{2,1,0:T(8,128)(2,1)} %refs_0_.2), channel_id=1, source_target_pairs={{0,1},{1,0},{2,3},{3,2},{4,5},{5,4},{6,7},{7,6},{8,9},{9,8},{10,11... | collective-permute-start | bytes 4718600 | tf_op jit(solution)/shard_map/ppermute | solution.py:706
  1.2 18.2 %collective-permute-start.1 = (bf16[2,512,768]{2,1,0:T(8,128)(2,1)}, bf16[2,512,768]{2,1,0:T(8,128)(2,1)S(1)}, u32[]{:S(2)}, u32[]{:S(2)}) collective-permute-start(bf16[2,512,768]{2,1,0:T(8,128)(2,1)} %refs_5_.6), channel_id=1, source_target_pairs={{0,1},{1,0},{2,3},{3,2},{4,5},{5,4},{6,7},{7,6},{8,9},{9,8},{10,11... | collective-permute-start | bytes 4718600 | tf_op jit(solution)/shard_map/ppermute | solution.py:706
  9.5 9.9 %collective-permute-start.2 = (f32[9,192]{1,0:T(8,128)S(1)}, f32[9,192]{1,0:T(8,128)S(1)}, u32[]{:S(2)}, u32[]{:S(2)}) collective-permute-start(f32[9,192]{1,0:T(8,128)S(1)} %reshape.39), channel_id=1, source_target_pairs={{0,1},{1,0},{2,3},{3,2},{4,5},{5,4},{6,7},{7,6},{8,9},{9,8},{10,11... | collective-permute-start | bytes 20744 | tf_op jit(solution)/shard_map/ppermute | solution.py:838
  9.9 9.4 %collective-permute-start.3 = (f32[9,192]{1,0:T(8,128)S(1)}, f32[9,192]{1,0:T(8,128)S(1)}, u32[]{:S(2)}, u32[]{:S(2)}) collective-permute-start(f32[9,192]{1,0:T(8,128)S(1)} %reshape.39), channel_id=1, source_target_pairs={{0,2},{1,3},{2,0},{3,1},{4,6},{5,7},{6,4},{7,5},{8,10},{9,11},{10,... | collective-permute-start | bytes 20744 | tf_op jit(solution)/shard_map/ppermute | solution.py:838
  12.5 6.9 %collective-permute-start.4 = (f32[9,192]{1,0:T(8,128)S(1)}, f32[9,192]{1,0:T(8,128)S(1)}, u32[]{:S(2)}, u32[]{:S(2)}) collective-permute-start(f32[9,192]{1,0:T(8,128)S(1)} %reshape.39), channel_id=1, source_target_pairs={{0,3},{1,2},{2,1},{3,0},{4,7},{5,6},{6,5},{7,4},{8,11},{9,10},{10,... | collective-permute-start | bytes 20744 | tf_op jit(solution)/shard_map/ppermute | solution.py:838
  19.4 26.8 %copy-start.14 = (bf16[2,512,768]{2,1,0:T(8,128)(2,1)}, bf16[2,512,768]{2,1,0:T(8,128)(2,1)S(1)}, u32[]{:S(2)}) copy-start(bf16[2,512,768]{2,1,0:T(8,128)(2,1)S(1)} %collective-permute-done.1.refs_6_) | copy-start | bytes 4718596
  63.6 14.5 %collective-permute-start.5 = (bf16[8,2,96,768]{3,2,1,0:T(8,128)(2,1)}, bf16[8,2,96,768]{3,2,1,0:T(8,128)(2,1)S(1)}, u32[]{:S(2)}, u32[]{:S(2)}) collective-permute-start(bf16[8,2,96,768]{3,2,1,0:T(8,128)(2,1)} %get-tuple-element.131), channel_id=1, source_target_pairs={{0,1},{1,0},{2,3},{3,2},{4,5},{5,4},{6,7},{7,6},{8,9},{9,8},{10,11... | collective-permute-start | bytes 7077896 | tf_op jit(solution)/shard_map/ppermute | solution.py:715
  78.1 18.7 %copy-start.3 = (bf16[8,2,96,768]{3,2,1,0:T(8,128)(2,1)}, bf16[8,2,96,768]{3,2,1,0:T(8,128)(2,1)S(1)}, u32[]{:S(2)}) copy-start(bf16[8,2,96,768]{3,2,1,0:T(8,128)(2,1)S(1)} %collective-permute-done.5) | copy-start | bytes 7077892
  80.3 16.4 %collective-permute-start.6 = (bf16[4,2,96,768]{3,2,1,0:T(8,128)(2,1)S(1)}, bf16[4,2,96,768]{3,2,1,0:T(8,128)(2,1)}, u32[]{:S(2)}, u32[]{:S(2)}) collective-permute-start(bf16[4,2,96,768]{3,2,1,0:T(8,128)(2,1)S(1)} %slice_add_fusion.2), channel_id=1, source_target_pairs={{0,4},{1,3},{2,6},{3,1},{4,0},{5,7},{6,2},{7,5},{8,12},{9,11},{10,... | collective-permute-start | bytes 3538952 | tf_op jit(solution)/shard_map/ppermute | solution.py:715
  98.2 18.5 %collective-permute-start.8 = (bf16[8,2,96,768]{3,2,1,0:T(8,128)(2,1)}, bf16[8,2,96,768]{3,2,1,0:T(8,128)(2,1)S(1)}, u32[]{:S(2)}, u32[]{:S(2)}) collective-permute-start(bf16[8,2,96,768]{3,2,1,0:T(8,128)(2,1)} %get-tuple-element.145), channel_id=1, source_target_pairs={{0,1},{1,0},{2,3},{3,2},{4,5},{5,4},{6,7},{7,6},{8,9},{9,8},{10,11... | collective-permute-start | bytes 7077896 | tf_op jit(solution)/shard_map/ppermute | solution.py:715
  98.3 16.2 %collective-permute-start.7 = (bf16[2,2,96,768]{3,2,1,0:T(8,128)(2,1)S(1)}, bf16[2,2,96,768]{3,2,1,0:T(8,128)(2,1)S(1)}, u32[]{:S(2)}, u32[]{:S(2)}) collective-permute-start(bf16[2,2,96,768]{3,2,1,0:T(8,128)(2,1)S(1)} %add_convert_fusion.2), channel_id=1, source_target_pairs={{0,2},{1,5},{2,0},{3,7},{4,6},{5,1},{6,4},{7,3},{8,10},{9,13},{10,... | collective-permute-start | bytes 1769480 | tf_op jit(solution)/shard_map/ppermute | solution.py:715
  118.2 16.4 %collective-permute-start.10 = (bf16[4,2,96,768]{3,2,1,0:T(8,128)(2,1)S(1)}, bf16[4,2,96,768]{3,2,1,0:T(8,128)(2,1)}, u32[]{:S(2)}, u32[]{:S(2)}) collective-permute-start(bf16[4,2,96,768]{3,2,1,0:T(8,128)(2,1)S(1)} %slice_add_fusion.1), channel_id=1, source_target_pairs={{0,4},{1,3},{2,6},{3,1},{4,0},{5,7},{6,2},{7,5},{8,12},{9,11},{10,... | collective-permute-start | bytes 3538952 | tf_op jit(solution)/shard_map/ppermute | solution.py:715
  119.7 9.5 %collective-permute-start.9 = (bf16[1,2,96,768]{3,2,1,0:T(8,128)(2,1)}, bf16[1,2,96,768]{3,2,1,0:T(8,128)(2,1)}, u32[]{:S(2)}, u32[]{:S(2)}) collective-permute-start(bf16[1,2,96,768]{3,2,1,0:T(8,128)(2,1)} %add_convert_fusion.8), channel_id=1, source_target_pairs={{0,8},{1,9},{2,10},{3,11},{4,12},{5,13},{6,14},{7,15},{8,0},{9,1},... | collective-permute-start | bytes 884744 | tf_op jit(solution)/shard_map/ppermute | solution.py:715
  121.3 15.5 %collective-permute-start.11 = (bf16[512,768]{1,0:T(8,128)(2,1)}, bf16[512,768]{1,0:T(8,128)(2,1)}, u32[]{:S(2)}, u32[]{:S(2)}) collective-permute-start(bf16[512,768]{1,0:T(8,128)(2,1)} %get-tuple-element.150), channel_id=1, source_target_pairs={{0,1},{1,0},{2,3},{3,2},{4,5},{5,4},{6,7},{7,6},{8,9},{9,8},{10,11... | collective-permute-start | bytes 2359304 | tf_op jit(solution)/shard_map/ppermute | solution.py:715
  136.8 22.9 %collective-permute-start.13 = (bf16[2,2,96,768]{3,2,1,0:T(8,128)(2,1)}, bf16[2,2,96,768]{3,2,1,0:T(8,128)(2,1)S(1)}, u32[]{:S(2)}, u32[]{:S(2)}) collective-permute-start(bf16[2,2,96,768]{3,2,1,0:T(8,128)(2,1)} %add_convert_fusion.1), channel_id=1, source_target_pairs={{0,2},{1,5},{2,0},{3,7},{4,6},{5,1},{6,4},{7,3},{8,10},{9,13},{10,... | collective-permute-start | bytes 1769480 | tf_op jit(solution)/shard_map/ppermute | solution.py:715
  137.0 21.7 %collective-permute-start.12 = (bf16[1,2,96,768]{3,2,1,0:T(8,128)(2,1)}, bf16[1,2,96,768]{3,2,1,0:T(8,128)(2,1)S(1)}, u32[]{:S(2)}, u32[]{:S(2)}) collective-permute-start(bf16[1,2,96,768]{3,2,1,0:T(8,128)(2,1)} %add_convert_fusion.7), channel_id=1, source_target_pairs={{0,16},{1,17},{2,18},{3,19},{4,20},{5,21},{6,22},{7,23},{8,24},{9,... | collective-permute-start | bytes 884744 | tf_op jit(solution)/shard_map/ppermute | solution.py:715
  160.9 21.1 %collective-permute-start.15 = (bf16[1,2,96,768]{3,2,1,0:T(8,128)(2,1)S(1)}, bf16[1,2,96,768]{3,2,1,0:T(8,128)(2,1)}, u32[]{:S(2)}, u32[]{:S(2)}) collective-permute-start(bf16[1,2,96,768]{3,2,1,0:T(8,128)(2,1)S(1)} %add_convert_fusion.6), channel_id=1, source_target_pairs={{0,8},{1,9},{2,10},{3,11},{4,12},{5,13},{6,14},{7,15},{8,0},{9,1},... | collective-permute-start | bytes 884744 | tf_op jit(solution)/shard_map/ppermute | solution.py:715
  162.6 20.8 %collective-permute-start.14 = (bf16[1,2,96,768]{3,2,1,0:T(8,128)(2,1)S(1)}, bf16[1,2,96,768]{3,2,1,0:T(8,128)(2,1)}, u32[]{:S(2)}, u32[]{:S(2)}) collective-permute-start(bf16[1,2,96,768]{3,2,1,0:T(8,128)(2,1)S(1)} %add.182), channel_id=1, source_target_pairs={{0,8},{1,9},{2,10},{3,11},{4,12},{5,13},{6,14},{7,15},{8,0},{9,1},... | collective-permute-start | bytes 884744 | tf_op jit(solution)/shard_map/ppermute | solution.py:715
  184.3 16.4 %collective-permute-start.16 = (bf16[2,2,96,768]{3,2,1,0:T(8,128)(2,1)S(1)}, bf16[2,2,96,768]{3,2,1,0:T(8,128)(2,1)S(1)}, u32[]{:S(2)}, u32[]{:S(2)}) collective-permute-start(bf16[2,2,96,768]{3,2,1,0:T(8,128)(2,1)S(1)} %pad_maximum_fusion.2), channel_id=1, source_target_pairs={{0,2},{1,5},{2,0},{3,7},{4,6},{5,1},{6,4},{7,3},{8,10},{9,13},{10,... | collective-permute-start | bytes 1769480 | tf_op jit(solution)/shard_map/ppermute | solution.py:715
  185.9 14.0 %collective-permute-start.17 = (bf16[1,2,96,768]{3,2,1,0:T(8,128)(2,1)S(1)}, bf16[1,2,96,768]{3,2,1,0:T(8,128)(2,1)S(1)}, u32[]{:S(2)}, u32[]{:S(2)}) collective-permute-start(bf16[1,2,96,768]{3,2,1,0:T(8,128)(2,1)S(1)} %add_convert_fusion.5), channel_id=1, source_target_pairs={{0,16},{1,17},{2,18},{3,19},{4,20},{5,21},{6,22},{7,23},{8,24},{9,... | collective-permute-start | bytes 884744 | tf_op jit(solution)/shard_map/ppermute | solution.py:715
  200.8 17.0 %copy-start.1 = (bf16[4,2,96,768]{3,2,1,0:T(8,128)(2,1)}, bf16[4,2,96,768]{3,2,1,0:T(8,128)(2,1)S(1)}, u32[]{:S(2)}) copy-start(bf16[4,2,96,768]{3,2,1,0:T(8,128)(2,1)S(1)} %pad_maximum_fusion.refs_0_) | copy-start | bytes 3538948
  200.8 12.2 %collective-permute-start.18 = (bf16[8,192,768]{2,1,0:T(8,128)(2,1)}, bf16[8,192,768]{2,1,0:T(8,128)(2,1)}, u32[]{:S(2)}, u32[]{:S(2)}) collective-permute-start(bf16[8,192,768]{2,1,0:T(8,128)(2,1)} %get-tuple-element.179), channel_id=1, source_target_pairs={{0,1},{1,0},{2,3},{3,2},{4,5},{5,4},{6,7},{7,6},{8,9},{9,8},{10,11... | collective-permute-start | bytes 7077896 | tf_op jit(solution)/shard_map/ppermute | solution.py:715
  200.9 16.4 %collective-permute-start.19 = (bf16[4,2,96,768]{3,2,1,0:T(8,128)(2,1)S(1)}, bf16[4,2,96,768]{3,2,1,0:T(8,128)(2,1)}, u32[]{:S(2)}, u32[]{:S(2)}) collective-permute-start(bf16[4,2,96,768]{3,2,1,0:T(8,128)(2,1)S(1)} %pad_maximum_fusion.refs_0_), channel_id=1, source_target_pairs={{0,4},{1,3},{2,6},{3,1},{4,0},{5,7},{6,2},{7,5},{8,12},{9,11},{10,... | collective-permute-start | bytes 3538952 | tf_op jit(solution)/shard_map/ppermute | solution.py:715
  201.5 10.7 %copy-start.13 = (f32[2,768]{1,0:T(2,128)S(1)}, f32[2,768]{1,0:T(2,128)}, u32[]{:S(2)}) copy-start(f32[2,768]{1,0:T(2,128)} %get-tuple-element.184) | copy-start | bytes 18436
  201.5 11.6 %copy-start.2 = (bf16[8,192,768]{2,1,0:T(8,128)(2,1)S(1)}, bf16[8,192,768]{2,1,0:T(8,128)(2,1)}, u32[]{:S(2)}) copy-start(bf16[8,192,768]{2,1,0:T(8,128)(2,1)} %get-tuple-element.178) | copy-start | bytes 7077892
  214.5 21.8 %copy-start.9 = (bf16[1,2,96,768]{3,2,1,0:T(8,128)(2,1)S(1)}, bf16[1,2,96,768]{3,2,1,0:T(8,128)(2,1)}, u32[]{:S(2)}) copy-start(bf16[1,2,96,768]{3,2,1,0:T(8,128)(2,1)} %add.190) | copy-start | bytes 884740
  217.3 16.2 %collective-permute-start.20 = (bf16[4,192,768]{2,1,0:T(8,128)(2,1)S(1)}, bf16[4,192,768]{2,1,0:T(8,128)(2,1)S(1)}, u32[]{:S(2)}, u32[]{:S(2)}) collective-permute-start(bf16[4,192,768]{2,1,0:T(8,128)(2,1)S(1)} %slice_add_fusion), channel_id=1, source_target_pairs={{0,4},{1,3},{2,6},{3,1},{4,0},{5,7},{6,2},{7,5},{8,12},{9,11},{10,... | collective-permute-start | bytes 3538952 | tf_op jit(solution)/shard_map/ppermute | solution.py:715
  217.8 17.0 %collective-permute-start.22 = (bf16[4,2,96,768]{3,2,1,0:T(8,128)(2,1)S(1)}, bf16[4,2,96,768]{3,2,1,0:T(8,128)(2,1)S(1)}, u32[]{:S(2)}, u32[]{:S(2)}) collective-permute-start(bf16[4,2,96,768]{3,2,1,0:T(8,128)(2,1)S(1)} %pad_maximum_fusion.refs_0_), channel_id=1, source_target_pairs={{0,1},{1,0},{2,3},{3,2},{4,5},{5,4},{6,7},{7,6},{8,9},{9,8},{10,11... | collective-permute-start | bytes 3538952 | tf_op jit(solution)/shard_map/ppermute | solution.py:715
  217.9 16.8 %collective-permute-start.23 = (bf16[512,768]{1,0:T(8,128)(2,1)S(1)}, bf16[512,768]{1,0:T(8,128)(2,1)S(1)}, u32[]{:S(2)}, u32[]{:S(2)}) collective-permute-start(bf16[512,768]{1,0:T(8,128)(2,1)S(1)} %copy-done.15), channel_id=1, source_target_pairs={{0,1},{1,0},{2,3},{3,2},{4,5},{5,4},{6,7},{7,6},{8,9},{9,8},{10,11... | collective-permute-start | bytes 2359304 | tf_op jit(solution)/shard_map/ppermute | solution.py:715
  218.3 3.5 %collective-permute-start.21 = (f32[13,768]{1,0:T(8,128)S(1)}, f32[13,768]{1,0:T(8,128)S(1)}, u32[]{:S(2)}, u32[]{:S(2)}) collective-permute-start(f32[13,768]{1,0:T(8,128)S(1)} %pad_maximum_fusion.7), channel_id=1, source_target_pairs={{0,1},{1,0},{2,3},{3,2},{4,5},{5,4},{6,7},{7,6},{8,9},{9,8},{10,11... | collective-permute-start | bytes 119816 | tf_op jit(solution)/shard_map/ppermute | solution.py:715
  234.8 21.6 %copy-start.10 = (bf16[512,768]{1,0:T(8,128)(2,1)}, bf16[512,768]{1,0:T(8,128)(2,1)S(1)}, u32[]{:S(2)}) copy-start(bf16[512,768]{1,0:T(8,128)(2,1)S(1)} %collective-permute-done.23) | copy-start | bytes 2359300
  234.8 21.6 %copy-start.7 = (bf16[4,2,96,768]{3,2,1,0:T(8,128)(2,1)}, bf16[4,2,96,768]{3,2,1,0:T(8,128)(2,1)S(1)}, u32[]{:S(2)}) copy-start(bf16[4,2,96,768]{3,2,1,0:T(8,128)(2,1)S(1)} %collective-permute-done.22.refs_2_) | copy-start | bytes 3538948
  234.8 12.1 %collective-permute-start.27 = (bf16[4,2,96,768]{3,2,1,0:T(8,128)(2,1)}, bf16[4,2,96,768]{3,2,1,0:T(8,128)(2,1)S(1)}, u32[]{:S(2)}, u32[]{:S(2)}) collective-permute-start(bf16[4,2,96,768]{3,2,1,0:T(8,128)(2,1)} %collective-permute-done.19.refs_1_), channel_id=1, source_target_pairs={{0,1},{1,0},{2,3},{3,2},{4,5},{5,4},{6,7},{7,6},{8,9},{9,8},{10,11... | collective-permute-start | bytes 3538952 | tf_op jit(solution)/shard_map/ppermute | solution.py:715
  234.9 10.9 %collective-permute-start.24 = (bf16[2,192,768]{2,1,0:T(8,128)(2,1)S(1)}, bf16[2,192,768]{2,1,0:T(8,128)(2,1)S(1)}, u32[]{:S(2)}, u32[]{:S(2)}) collective-permute-start(bf16[2,192,768]{2,1,0:T(8,128)(2,1)S(1)} %add_convert_fusion), channel_id=1, source_target_pairs={{0,2},{1,5},{2,0},{3,7},{4,6},{5,1},{6,4},{7,3},{8,10},{9,13},{10,... | collective-permute-start | bytes 1769480 | tf_op jit(solution)/shard_map/ppermute | solution.py:715
  236.3 8.2 %collective-permute-start.25 = (bf16[1,2,96,768]{3,2,1,0:T(8,128)(2,1)S(1)}, bf16[1,2,96,768]{3,2,1,0:T(8,128)(2,1)S(1)}, u32[]{:S(2)}, u32[]{:S(2)}) collective-permute-start(bf16[1,2,96,768]{3,2,1,0:T(8,128)(2,1)S(1)} %copy-done.9), channel_id=1, source_target_pairs={{0,8},{1,9},{2,10},{3,11},{4,12},{5,13},{6,14},{7,15},{8,0},{9,1},... | collective-permute-start | bytes 884744 | tf_op jit(solution)/shard_map/ppermute | solution.py:715
  236.3 9.5 %collective-permute-start.26 = (f32[13,768]{1,0:T(8,128)S(1)}, f32[13,768]{1,0:T(8,128)S(1)}, u32[]{:S(2)}, u32[]{:S(2)}) collective-permute-start(f32[13,768]{1,0:T(8,128)S(1)} %add.194), channel_id=1, source_target_pairs={{0,2},{1,3},{2,0},{3,1},{4,6},{5,7},{6,4},{7,5},{8,10},{9,11},{10,... | collective-permute-start | bytes 119816 | tf_op jit(solution)/shard_map/ppermute | solution.py:715
  246.9 9.9 %collective-permute-start.29 = (bf16[2,2,96,768]{3,2,1,0:T(8,128)(2,1)S(1)}, bf16[2,2,96,768]{3,2,1,0:T(8,128)(2,1)S(1)}, u32[]{:S(2)}, u32[]{:S(2)}) collective-permute-start(bf16[2,2,96,768]{3,2,1,0:T(8,128)(2,1)S(1)} %pad_maximum_fusion.3), channel_id=1, source_target_pairs={{0,2},{1,5},{2,0},{3,7},{4,6},{5,1},{6,4},{7,3},{8,10},{9,13},{10,... | collective-permute-start | bytes 1769480 | tf_op jit(solution)/shard_map/ppermute | solution.py:715
  248.4 6.9 %collective-permute-start.28 = (bf16[1,192,768]{2,1,0:T(8,128)(2,1)S(1)}, bf16[1,192,768]{2,1,0:T(8,128)(2,1)S(1)}, u32[]{:S(2)}, u32[]{:S(2)}) collective-permute-start(bf16[1,192,768]{2,1,0:T(8,128)(2,1)S(1)} %add_convert_fusion.4), channel_id=1, source_target_pairs={{0,8},{1,9},{2,10},{3,11},{4,12},{5,13},{6,14},{7,15},{8,0},{9,1},... | collective-permute-start | bytes 884744 | tf_op jit(solution)/shard_map/ppermute | solution.py:715
  248.4 4.6 %collective-permute-start.30 = (f32[13,768]{1,0:T(8,128)S(1)}, f32[13,768]{1,0:T(8,128)S(1)}, u32[]{:S(2)}, u32[]{:S(2)}) collective-permute-start(f32[13,768]{1,0:T(8,128)S(1)} %add.201), channel_id=1, source_target_pairs={{0,4},{1,5},{2,6},{3,7},{4,0},{5,1},{6,2},{7,3},{8,12},{9,13},{10,... | collective-permute-start | bytes 119816 | tf_op jit(solution)/shard_map/ppermute | solution.py:715
  257.0 17.2 %copy-start = (bf16[4,2,96,768]{3,2,1,0:T(8,128)(2,1)}, bf16[4,2,96,768]{3,2,1,0:T(8,128)(2,1)S(1)}, u32[]{:S(2)}) copy-start(bf16[4,2,96,768]{3,2,1,0:T(8,128)(2,1)S(1)} %pad_maximum_fusion.1.refs_0_) | copy-start | bytes 3538948
  257.0 17.1 %collective-permute-start.32 = (bf16[4,2,96,768]{3,2,1,0:T(8,128)(2,1)S(1)}, bf16[4,2,96,768]{3,2,1,0:T(8,128)(2,1)S(1)}, u32[]{:S(2)}, u32[]{:S(2)}) collective-permute-start(bf16[4,2,96,768]{3,2,1,0:T(8,128)(2,1)S(1)} %pad_maximum_fusion.1.refs_0_), channel_id=1, source_target_pairs={{0,4},{1,3},{2,6},{3,1},{4,0},{5,7},{6,2},{7,5},{8,12},{9,11},{10,... | collective-permute-start | bytes 3538952 | tf_op jit(solution)/shard_map/ppermute | solution.py:715
  257.7 16.3 %collective-permute-start.31 = (bf16[1,192,768]{2,1,0:T(8,128)(2,1)S(1)}, bf16[1,192,768]{2,1,0:T(8,128)(2,1)S(1)}, u32[]{:S(2)}, u32[]{:S(2)}) collective-permute-start(bf16[1,192,768]{2,1,0:T(8,128)(2,1)S(1)} %add_convert_fusion.3), channel_id=1, source_target_pairs={{0,16},{1,17},{2,18},{3,19},{4,20},{5,21},{6,22},{7,23},{8,24},{9,... | collective-permute-start | bytes 884744 | tf_op jit(solution)/shard_map/ppermute | solution.py:715
  259.4 10.4 %collective-permute-start.33 = (f32[13,768]{1,0:T(8,128)S(1)}, f32[13,768]{1,0:T(8,128)S(1)}, u32[]{:S(2)}, u32[]{:S(2)}) collective-permute-start(f32[13,768]{1,0:T(8,128)S(1)} %add.203), channel_id=1, source_target_pairs={{0,8},{1,9},{2,10},{3,11},{4,12},{5,13},{6,14},{7,15},{8,0},{9,1},... | collective-permute-start | bytes 119816 | tf_op jit(solution)/shard_map/ppermute | solution.py:715
  274.2 10.7 %collective-permute-start.36 = (bf16[4,2,96,768]{3,2,1,0:T(8,128)(2,1)S(1)}, bf16[4,2,96,768]{3,2,1,0:T(8,128)(2,1)}, u32[]{:S(2)}, u32[]{:S(2)}) collective-permute-start(bf16[4,2,96,768]{3,2,1,0:T(8,128)(2,1)S(1)} %pad_maximum_fusion.1.refs_0_), channel_id=1, source_target_pairs={{0,1},{1,0},{2,3},{3,2},{4,5},{5,4},{6,7},{7,6},{8,9},{9,8},{10,11... | collective-permute-start | bytes 3538952 | tf_op jit(solution)/shard_map/ppermute | solution.py:715
  274.3 10.6 %collective-permute-start.37 = (bf16[4,2,96,768]{3,2,1,0:T(8,128)(2,1)S(1)}, bf16[4,2,96,768]{3,2,1,0:T(8,128)(2,1)}, u32[]{:S(2)}, u32[]{:S(2)}) collective-permute-start(bf16[4,2,96,768]{3,2,1,0:T(8,128)(2,1)S(1)} %collective-permute-done.32.refs_1_), channel_id=1, source_target_pairs={{0,1},{1,0},{2,3},{3,2},{4,5},{5,4},{6,7},{7,6},{8,9},{9,8},{10,11... | collective-permute-start | bytes 3538952 | tf_op jit(solution)/shard_map/ppermute | solution.py:715
  274.7 10.0 %collective-permute-start.35 = (bf16[1,192,768]{2,1,0:T(8,128)(2,1)S(1)}, bf16[1,192,768]{2,1,0:T(8,128)(2,1)S(1)}, u32[]{:S(2)}, u32[]{:S(2)}) collective-permute-start(bf16[1,192,768]{2,1,0:T(8,128)(2,1)S(1)} %add.204), channel_id=1, source_target_pairs={{0,8},{1,9},{2,10},{3,11},{4,12},{5,13},{6,14},{7,15},{8,0},{9,1},... | collective-permute-start | bytes 884744 | tf_op jit(solution)/shard_map/ppermute | solution.py:715
  277.7 10.9 %collective-permute-start.34 = (f32[13,768]{1,0:T(8,128)}, f32[13,768]{1,0:T(8,128)S(1)}, u32[]{:S(2)}, u32[]{:S(2)}) collective-permute-start(f32[13,768]{1,0:T(8,128)} %add.205), channel_id=1, source_target_pairs={{0,16},{1,17},{2,18},{3,19},{4,20},{5,21},{6,22},{7,23},{8,24},{9,... | collective-permute-start | bytes 119816 | tf_op jit(solution)/shard_map/ppermute | solution.py:715
  284.9 14.9 %collective-permute-start.38 = (bf16[2,192,768]{2,1,0:T(8,128)(2,1)S(1)}, bf16[2,192,768]{2,1,0:T(8,128)(2,1)S(1)}, u32[]{:S(2)}, u32[]{:S(2)}) collective-permute-start(bf16[2,192,768]{2,1,0:T(8,128)(2,1)S(1)} %pad_maximum_fusion.4), channel_id=1, source_target_pairs={{0,4},{1,5},{2,6},{3,7},{4,0},{5,1},{6,2},{7,3},{8,12},{9,13},{10,... | collective-permute-start | bytes 1769480 | tf_op jit(solution)/shard_map/ppermute | solution.py:715
  (7 other events, 35.0 us)
